TPU v7x, 32 devices: a whole 2x2x4 slice. The times are simulated.
32 devices in a mesh: groups: 2 (over y), vel: 4 (over z), cell: 2 (over x), sub: 2 (over core).
Axes of the slice: x: 2, y: 2, z: 4, core: 2. Of those that a mesh axis runs over, the one named last changes fastest.
Arguments:
- density: bfloat16 [768, 110592], P(('groups', 'cell', 'sub'), 'vel'), parts along dimension 0, may hold values from 0.5 to 1.5
- coder: bfloat16 [110592, 512], P('vel'), may hold values from -0.01953125 to 0.01953125
- w_latent: bfloat16 [512, 512], replicated, may hold values from -0.25 to 0.25
- b_latent: float32 [512], replicated, may hold values from -3 to 3
- restitution: float32 [768], P(('groups', 'cell', 'sub')), parts along dimension 0, may hold values from 0.3 to 0.95
- inflow: float32 [221184], P(('groups', 'vel')), parts along dimension 0, may hold values from 0.5 to 1.5
- flags: int32 [8], P('groups'), parts along dimension 0, may hold values from 0 to 1, as said below
- blocks: int32 [192], P(('groups', 'vel')), parts along dimension 0, may hold values from 0 to 95, each once
Outputs:
- density_out: bfloat16 [768, 110592], P(('groups', 'cell', 'sub'), 'vel'), parts along dimension 0
There are 2 independent parts, one for each index of `groups`. A program takes and returns all parts, laid end to end along the dimension named above; an argument that names none is the same for every part. Nothing has to cross between parts.
Inputs may be any that keep to these rules, and one draw needn't show every extreme that they name: flags[b] = 1 joins block b of 96 cells to block b - 1 (block 0 to the last block); 0 makes that boundary an inflow boundary. Every draw holds both values. A permutation of the velocity blocks.
All inputs are finite; a program needn't handle non-finite values.
Results may differ from a plain program's by a relative error of at most 0.007.
Values may be sent and summed in bfloat16 or wider, within the bound.
No kernel may reach another device: no remote copies, remote signals or barrier semaphores. Data moves between devices by JAX's collectives and lax.ppermute only.
A program may use at most 128 MiB of HBM per device.

v0:
```python
import math

import jax
import jax.numpy as jnp
import numpy as np
from jax import lax
from jax.sharding import PartitionSpec as P

VGRID = 48
LATENT = 512
VBLOCKS = 96
STEPS = 2
VELS = 110592


SINK_RATE = 0.5
COURANT = 0.9


def extended(cells, sides, width):
    for axis, dim in sides:
        count = lax.axis_size(axis)
        head = lax.slice_in_dim(cells, 0, width, axis=dim)
        tail = lax.slice_in_dim(cells, cells.shape[dim] - width, cells.shape[dim], axis=dim)
        cells = jnp.concatenate(
            [
                lax.ppermute(tail, axis, [(i, (i + 1) % count) for i in range(count)]),
                cells,
                lax.ppermute(head, axis, [((i + 1) % count, i) for i in range(count)]),
            ],
            axis=dim,
        )
    return cells


def grid_moments():
    centres = (2.0 * np.arange(VGRID) + 1.0 - VGRID) / VGRID
    second = float(np.sum(centres**2))
    fourth = float(np.sum(centres**4))
    number = float(VGRID)
    total = number**3
    cross = 3.0 * number * number * second
    quartic = 3.0 * number * number * fourth + 6.0 * number * second * second
    square = number * number * second
    return (total, cross, quartic, square)


def component(number):
    return (2 * number + 1 - VGRID).astype(jnp.float32) / VGRID


def velocity_rows(blocks):
    width = VELS // VBLOCKS
    number = (blocks[:, None] * width + jnp.arange(width, dtype=jnp.int32)[None, :]).reshape(-1)
    along_x = component(number // (VGRID * VGRID))
    along_y = component(number // VGRID % VGRID)
    along_z = component(number % VGRID)
    kinetic = along_x * along_x + along_y * along_y + along_z * along_z
    return jnp.stack([jnp.ones_like(along_x), along_x, along_y, along_z, kinetic])


def advect(padded, courant):
    length = padded.shape[0] - 4
    magnitude = jnp.abs(courant)
    lower = padded[0 : length + 1]
    centre = padded[1 : length + 2]
    upper = padded[2 : length + 3]
    beyond = padded[3 : length + 4]
    upwind = (1.0 - magnitude) / 2.0
    curved = (1.0 - magnitude * magnitude) / 6.0
    forward = centre + upwind * (upper - centre) - curved * (upper - 2.0 * centre + lower)
    backward = upper + upwind * (centre - upper) - curved * (centre - 2.0 * upper + beyond)
    flux = courant * jnp.where(courant >= 0.0, forward, backward)
    return padded[2 : length + 2] - (flux[1:] - flux[:-1])


def project(fstar, collision, moments, energy_sum, restitution, basis):
    total, cross, quartic, square = grid_moments()
    sink = -SINK_RATE * (1.0 - restitution * restitution) * energy_sum
    excess = moments[4] - sink
    determinant = total * quartic - cross * cross
    mass_mult = (quartic * moments[0] - cross * excess) / determinant
    energy_mult = (total * excess - cross * moments[0]) / determinant
    weights = jnp.stack(
        [mass_mult, moments[1] / square, moments[2] / square, moments[3] / square, energy_mult]
    )
    correction = lax.dot_general(
        weights, basis, (((0,), (0,)), ((), ())), precision=lax.Precision.HIGHEST
    )
    return fstar + (collision - correction)


def latent_layer(encoded, w_latent, b_latent):
    mixed = jnp.dot(encoded.astype(jnp.bfloat16), w_latent, preferred_element_type=jnp.float32)
    return jnp.tanh(mixed + b_latent).astype(jnp.bfloat16)


def body(density, coder, w_latent, b_latent, restitution, inflow, flags, blocks):
    basis = velocity_rows(blocks)
    courant = COURANT * basis[1]
    sub_count = lax.axis_size("sub")
    position = lax.axis_index("cell") * sub_count + lax.axis_index("sub")
    block_count = lax.axis_size("cell") * sub_count
    open_left = lax.dynamic_index_in_dim(flags, position, 0, keepdims=False) == 1
    open_right = (
        lax.dynamic_index_in_dim(flags, (position + 1) % block_count, 0, keepdims=False) == 1
    )
    scale = math.sqrt(VELS / LATENT)
    state = density.astype(jnp.float32)
    for section_index in range(STEPS):
        padded = extended(state, ((("cell", "sub"), 0),), 2)
        lead_rows = jnp.where(open_left, padded[:2], inflow[None, :])
        tail_rows = jnp.where(open_right, padded[-2:], inflow[None, :])
        padded = jnp.concatenate([lead_rows, padded[2:-2], tail_rows], 0)
        fstar = advect(padded, courant)
        coarse = fstar.astype(jnp.bfloat16)
        partial_code = jnp.dot(coarse, coder, preferred_element_type=jnp.float32)
        partial_energy = jnp.dot(fstar, basis[4], precision=lax.Precision.HIGHEST)
        encoded, energy_sum = lax.psum((partial_code, partial_energy), "vel")
        active = latent_layer(encoded, w_latent, b_latent)
        collision = scale * lax.dot_general(
            active, coder, (((1,), (1,)), ((), ())), preferred_element_type=jnp.float32
        )
        local_part = lax.dot_general(
            basis, collision, (((1,), (1,)), ((), ())), precision=lax.Precision.HIGHEST
        )
        moments = lax.psum(local_part, "vel")
        state = project(fstar, collision, moments, energy_sum, restitution, basis)
    return state.astype(jnp.bfloat16)


def solution(mesh):
    return jax.shard_map(
        body,
        mesh=mesh,
        in_specs=(
            P(("groups", "cell", "sub"), "vel"),
            P("vel", None),
            P(),
            P(),
            P(("groups", "cell", "sub")),
            P(("groups", "vel")),
            P("groups"),
            P(("groups", "vel")),
        ),
        out_specs=P(("groups", "cell", "sub"), "vel"),
        check_vma=False,
    )
```

profile of v0, /device:TPU:0, one launch (start us, length us, event | category | flops | bytes accessed | tf_op | source)
XLA Modules:
  0.0 265.2 jit_solution(6619362317704256406)
XLA Ops:
  0.0 1.3 fusion.80
  1.4 0.6 collective-permute-start
  1.9 2.0 collective-permute-start.1
  3.9 0.7 broadcast_multiply_fusion
  5.9 1.4 multiply_add_fusion
  7.4 7.5 %convert_element_type.81 = f32[96,27648]{1,0:T(8,128)} convert(bf16[96,27648]{1,0:T(8,128)(2,1)} %param.8) | non-fusion elementwise | flops 2654208 | bytes 15925248 | tf_op jit(solution)/shard_map/convert_element_type | solution.py:109
  14.9 0.6 fusion.81
  16.8 1.1 stack.14
  18.0 0.2 broadcast_select_fusion.3
  18.2 18.1 %fusion.15 = f32[97,27648]{1,0:T(8,128)S(1)} fusion(f32[2,27648]{1,0:T(2,128)S(1)} %get-tuple-element.28, f32[96,27648]{1,0:T(8,128)} %convert_element_type.81, f32[2,27648]{1,0:T(2,128)S(1)} %get-tuple-element.27, f32[27648]{0:T(1024)S(1)} %get-tuple-element.26, f32[27648]{0:T(1024)S(1)} %get-tuple-element.25, f32[27648]{0:T(1024)S(1)} %get-tuple-element.18, ...), kind=kLoop, calls=%fused_computation.24 | loop fusion | flops 59000832 | bytes 22146048 | tf_op jit(solution)/shard_map/mul | solution.py:73
  36.4 1.8 fusion.20
  38.2 4.0 %copy-done.1 = f32[96,27648]{1,0:T(8,128)} copy-done((f32[96,27648]{1,0:T(8,128)}, f32[96,27648]{1,0:T(8,128)S(1)}, u32[]{:S(2)}) %copy-start.1) | copy-done | bytes 10616856
  42.2 8.3 %convolution_bitcast_fusion.1 = f32[96]{0:T(128)S(1)} fusion(f32[96,27648]{1,0:T(8,128)S(1)} %fusion.20, f32[27648,1]{0,1:T(1,128)S(1)} %bitcast.88), kind=kOutput, calls=%fused_computation.46 | convolution fusion | flops 31850496 | bytes 10727808 | tf_op jit(solution)/shard_map/dot_general | solution.py:118
  50.5 14.5 %fusion.23 = f32[96,512]{1,0:T(8,128)S(1)} fusion(bf16[27648,512]{1,0:T(8,128)(2,1)} %param.9, f32[96,27648]{1,0:T(8,128)} %copy-done.1), kind=kOutput, calls=%fused_computation.37 | convolution fusion | flops 2720563200 | bytes 39124992 | tf_op jit(solution)/shard_map/dot_general | solution.py:117
  65.0 23.7 %all-reduce.4 = bf16[96,512]{1,0:T(8,128)(2,1)S(1)} all-reduce(f32[96,512]{1,0:T(8,128)S(1)} %fusion.23), channel_id=1, replica_groups=mesh['groups'=2,'vel'=4,'cell'=2,'sub'=2] {'vel'}, use_global_device_ids=true, to_apply=%region_0.1 | all-reduce | flops 49152 | bytes 294912 | tf_op jit(solution)/shard_map/psum | solution.py:119
  88.7 17.9 %convolution_multiply_fusion.1 = f32[96,27648]{1,0:T(8,128)} fusion(bf16[27648,512]{1,0:T(8,128)(2,1)} %param.9, bf16[512,512]{1,0:T(8,128)(2,1)S(1)} %copy-done, f32[512]{0:T(512)S(1)} %copy-done.4, bf16[96,512]{1,0:T(8,128)(2,1)S(1)} %all-reduce.4), kind=kOutput, calls=%fused_computation.1 | convolution fusion | flops 2770993152 | bytes 39553024 | tf_op jit(solution)/shard_map/dot_general | solution.py:121
  106.7 10.9 %fusion.82 = f32[5,96]{1,0:T(8,128)S(1)} fusion(f32[5,27648]{1,0:T(8,128)S(1)} %stack.14, f32[96,27648]{1,0:T(8,128)} %convolution_multiply_fusion.1), kind=kOutput, calls=%fused_computation.129 | convolution fusion | flops 159252480 | bytes 11171712 | tf_op jit(solution)/shard_map/dot_general | solution.py:124
  117.6 8.5 %all-reduce.1 = (f32[96]{0:T(128)S(1)}, f32[5,96]{1,0:T(8,128)S(1)}) all-reduce(f32[96]{0:T(128)S(1)} %convolution_bitcast_fusion.1, f32[5,96]{1,0:T(8,128)S(1)} %fusion.82), channel_id=1, replica_groups=mesh['groups'=2,'vel'=4,'cell'=2,'sub'=2] {'vel'}, use_global_device_ids=true, to_apply=%region_2.3 | all-reduce | flops 576 | bytes 4608 | tf_op jit(solution)/shard_map/psum | solution.py:119
  126.2 12.3 %fusion.1 = f32[96,27648]{1,0:T(8,128)S(1)} fusion(f32[96,27648]{1,0:T(8,128)} %copy-done.1, f32[96,27648]{1,0:T(8,128)} %convolution_multiply_fusion.1, f32[5,96]{1,0:T(8,128)S(1)} %stack.34, f32[5,27648]{1,0:T(8,128)S(1)} %stack.14), kind=kOutput, calls=%fused_computation.5 | convolution fusion | flops 164560896 | bytes 32405376 | tf_op jit(solution)/shard_map/dot_general | solution.py:87
  138.8 1.7 collective-permute-start.3
  140.5 4.5 %collective-permute-done.2 = f32[2,27648]{1,0:T(2,128)S(1)} collective-permute-done((f32[2,27648]{1,0:T(2,128)S(1)}, f32[2,27648]{1,0:T(2,128)S(1)}, u32[]{:S(2)}, u32[]{:S(2)}) %collective-permute-start.2) | collective-permute-done | bytes 221216 | tf_op jit(solution)/shard_map/ppermute | solution.py:27
  145.2 0.2 broadcast_select_fusion.2
  145.4 11.2 %fusion.7 = f32[97,27648]{1,0:T(8,128)} fusion(f32[2,27648]{1,0:T(2,128)S(1)} %get-tuple-element.24, f32[96,27648]{1,0:T(8,128)S(1)} %fusion.1, f32[2,27648]{1,0:T(2,128)S(1)} %get-tuple-element.23, f32[27648]{0:T(1024)S(1)} %get-tuple-element.26, f32[27648]{0:T(1024)S(1)} %get-tuple-element.25, f32[27648]{0:T(1024)S(1)} %get-tuple-element.18, ...), kind=kLoop, calls=%fused_computation.12 | loop fusion | flops 59000832 | bytes 22146048 | tf_op jit(solution)/shard_map/mul | solution.py:73
  156.6 8.2 %fusion.19 = f32[96,27648]{1,0:T(8,128)S(1)} fusion(f32[96,27648]{1,0:T(8,128)S(1)} %fusion.1, f32[97,27648]{1,0:T(8,128)} %fusion.7), kind=kLoop, calls=%fused_computation.32 | loop fusion | flops 5308416 | bytes 42467328 | tf_op jit(solution)/shard_map/sub | solution.py:74
  164.8 4.0 %copy-done.2 = f32[96,27648]{1,0:T(8,128)} copy-done((f32[96,27648]{1,0:T(8,128)}, f32[96,27648]{1,0:T(8,128)S(1)}, u32[]{:S(2)}) %copy-start.2) | copy-done | bytes 10616856
  168.8 8.3 %convolution_bitcast_fusion = f32[96]{0:T(128)S(1)} fusion(f32[96,27648]{1,0:T(8,128)S(1)} %fusion.19, f32[27648,1]{0,1:T(1,128)S(1)} %bitcast.89), kind=kOutput, calls=%fused_computation.45 | convolution fusion | flops 31850496 | bytes 10727808 | tf_op jit(solution)/shard_map/dot_general | solution.py:118
  177.1 14.5 %fusion.21 = f32[96,512]{1,0:T(8,128)S(1)} fusion(bf16[27648,512]{1,0:T(8,128)(2,1)} %param.9, f32[96,27648]{1,0:T(8,128)} %copy-done.2), kind=kOutput, calls=%fused_computation.35 | convolution fusion | flops 2720563200 | bytes 39124992 | tf_op jit(solution)/shard_map/dot_general | solution.py:117
  191.6 21.9 %all-reduce.5 = bf16[96,512]{1,0:T(8,128)(2,1)S(1)} all-reduce(f32[96,512]{1,0:T(8,128)S(1)} %fusion.21), channel_id=1, replica_groups=mesh['groups'=2,'vel'=4,'cell'=2,'sub'=2] {'vel'}, use_global_device_ids=true, to_apply=%region_3.4 | all-reduce | flops 49152 | bytes 294912 | tf_op jit(solution)/shard_map/psum | solution.py:119
  213.5 17.9 %convolution_multiply_fusion = f32[96,27648]{1,0:T(8,128)} fusion(bf16[27648,512]{1,0:T(8,128)(2,1)} %param.9, bf16[512,512]{1,0:T(8,128)(2,1)S(1)} %copy-done, bf16[96,512]{1,0:T(8,128)(2,1)S(1)} %all-reduce.5, f32[512]{0:T(512)S(1)} %copy-done.4), kind=kOutput, calls=%fused_computation | convolution fusion | flops 2770993152 | bytes 39553024 | tf_op jit(solution)/shard_map/dot_general | solution.py:121
  231.5 10.9 %fusion.83 = f32[5,96]{1,0:T(8,128)S(1)} fusion(f32[5,27648]{1,0:T(8,128)S(1)} %stack.14, f32[96,27648]{1,0:T(8,128)} %convolution_multiply_fusion), kind=kOutput, calls=%fused_computation.130 | convolution fusion | flops 159252480 | bytes 11171712 | tf_op jit(solution)/shard_map/dot_general | solution.py:124
  242.4 8.5 %all-reduce = (f32[96]{0:T(128)S(1)}, f32[5,96]{1,0:T(8,128)S(1)}) all-reduce(f32[96]{0:T(128)S(1)} %convolution_bitcast_fusion, f32[5,96]{1,0:T(8,128)S(1)} %fusion.83), channel_id=1, replica_groups=mesh['groups'=2,'vel'=4,'cell'=2,'sub'=2] {'vel'}, use_global_device_ids=true, to_apply=%region_5.6 | all-reduce | flops 576 | bytes 4608 | tf_op jit(solution)/shard_map/psum | solution.py:119
  251.0 14.1 %fusion.2 = bf16[96,27648]{1,0:T(8,128)(2,1)} fusion(f32[96,27648]{1,0:T(8,128)} %copy-done.2, f32[96,27648]{1,0:T(8,128)} %convolution_multiply_fusion, f32[5,96]{1,0:T(8,128)S(1)} %stack.37, f32[5,27648]{1,0:T(8,128)S(1)} %stack.14), kind=kOutput, calls=%fused_computation.6 | convolution fusion | flops 167215104 | bytes 27096960 | tf_op jit(solution)/shard_map/dot_general | solution.py:87
  (46 shorter events, 1.9 us)
Async XLA Ops:
  0.0 88.7 %copy-start = (bf16[512,512]{1,0:T(8,128)(2,1)S(1)}, bf16[512,512]{1,0:T(8,128)(2,1)}, u32[]{:S(2)}) copy-start(bf16[512,512]{1,0:T(8,128)(2,1)} %param.10) | copy-start | bytes 1572868
  0.0 14.9 %copy-start.5 = (s32[4]{0:T(128)S(1)}, s32[4]{0:T(128)}, u32[]{:S(2)}) copy-start(s32[4]{0:T(128)} %param.14) | copy-start | bytes 52
  0.0 18.0 %copy-start.3 = (f32[27648]{0:T(1024)S(1)}, f32[27648]{0:T(1024)}, u32[]{:S(2)}) copy-start(f32[27648]{0:T(1024)} %param.13) | copy-start | bytes 331780
  1.4 16.6 %collective-permute-start = (f32[2,27648]{1,0:T(2,128)S(1)}, f32[2,27648]{1,0:T(2,128)S(1)}, u32[]{:S(2)}, u32[]{:S(2)}) collective-permute-start(f32[2,27648]{1,0:T(2,128)S(1)} %get-tuple-element.21), channel_id=1, source_target_pairs={{0,1},{1,2},{2,3},{3,0},{4,5},{5,6},{6,7},{7,4},{8,9},{9,10},{10,1... | collective-permute-start | bytes 663560 | tf_op jit(solution)/shard_map/ppermute | solution.py:27
  1.9 16.0 %collective-permute-start.1 = (f32[2,27648]{1,0:T(2,128)S(1)}, f32[2,27648]{1,0:T(2,128)S(1)}, u32[]{:S(2)}, u32[]{:S(2)}) collective-permute-start(f32[2,27648]{1,0:T(2,128)S(1)} %get-tuple-element.22), channel_id=1, source_target_pairs={{1,0},{2,1},{3,2},{0,3},{5,4},{6,5},{7,6},{4,7},{9,8},{10,9},{11,1... | collective-permute-start | bytes 663560 | tf_op jit(solution)/shard_map/ppermute | solution.py:29
  18.2 18.2 %slice-start = ((s8[5308416]{0:T(1024)(128)(4,1)}), s8[4194304]{0:T(1024)(128)(4,1)S(1)}, s32[]{:S(2)}) async-start(s8[5308416]{0:T(1024)(128)(4,1)} %bitcast.86), calls=%async_computation | async-start | bytes 8388608
  18.2 18.2 %slice-start.1 = ((s8[5308416]{0:T(1024)(128)(4,1)}), s8[1114112]{0:T(1024)(128)(4,1)S(1)}, s32[]{:S(2)}) async-start(s8[5308416]{0:T(1024)(128)(4,1)} %bitcast.86), calls=%async_computation.1 | async-start | bytes 2228224
  38.2 4.1 %copy-start.1 = (f32[96,27648]{1,0:T(8,128)}, f32[96,27648]{1,0:T(8,128)S(1)}, u32[]{:S(2)}) copy-start(f32[96,27648]{1,0:T(8,128)S(1)} %fusion.20) | copy-start | bytes 31850500
  50.5 38.2 %copy-start.4 = (f32[512]{0:T(512)S(1)}, f32[512]{0:T(512)}, u32[]{:S(2)}) copy-start(f32[512]{0:T(512)} %param.11) | copy-start | bytes 6148
  106.7 19.5 %copy-start.6 = (f32[96]{0:T(128)S(1)}, f32[96]{0:T(128)}, u32[]{:S(2)}) copy-start(f32[96]{0:T(128)} %param.12) | copy-start | bytes 1156
  138.7 6.3 %collective-permute-start.2 = (f32[2,27648]{1,0:T(2,128)S(1)}, f32[2,27648]{1,0:T(2,128)S(1)}, u32[]{:S(2)}, u32[]{:S(2)}) collective-permute-start(f32[2,27648]{1,0:T(2,128)S(1)} %get-tuple-element.19), channel_id=1, source_target_pairs={{0,1},{1,2},{2,3},{3,0},{4,5},{5,6},{6,7},{7,4},{8,9},{9,10},{10,1... | collective-permute-start | bytes 663560 | tf_op jit(solution)/shard_map/ppermute | solution.py:27
  138.8 6.4 %collective-permute-start.3 = (f32[2,27648]{1,0:T(2,128)S(1)}, f32[2,27648]{1,0:T(2,128)S(1)}, u32[]{:S(2)}, u32[]{:S(2)}) collective-permute-start(f32[2,27648]{1,0:T(2,128)S(1)} %get-tuple-element.20), channel_id=1, source_target_pairs={{1,0},{2,1},{3,2},{0,3},{5,4},{6,5},{7,6},{4,7},{9,8},{10,9},{11,1... | collective-permute-start | bytes 663560 | tf_op jit(solution)/shard_map/ppermute | solution.py:29
  164.8 4.1 %copy-start.2 = (f32[96,27648]{1,0:T(8,128)}, f32[96,27648]{1,0:T(8,128)S(1)}, u32[]{:S(2)}) copy-start(f32[96,27648]{1,0:T(8,128)S(1)} %fusion.19) | copy-start | bytes 31850500
where the time goes:
time: 269 us; the launch traced here: 265 us
  matrix products  130 us (48%)
  blocking collectives  62.6 us (23%)
  other arithmetic  49.9 us (19%)
  local copies, waits for them, and re-layouts  12.2 us (5%)
  waiting for transfers between devices  4.67 us (2%)
  starting transfers between devices  4.32 us (2%)
    psum x4, blocking collectives, body(): encoded, energy_sum = lax.psum((partial_code, partial_energy), 'vel')  62.6 us
    dot_general x2, matrix products, body(): lax.dot_general(active, coder, (((1,), (1,)), ((), ())), preferred_elemen...  35.9 us
    mul x2, other arithmetic, advect(): flux = courant * jnp.where(courant >= 0.0, forward, backward)  29.3 us
    dot_general x2, matrix products, body(): partial_code = jnp.dot(coarse, coder, preferred_element_type=jnp.float32)  29 us
    dot_general x2, matrix products, project(): lax.dot_general(weights, basis, (((0,), (0,)), ((), ())), precision=lax.P...  26.4 us
    dot_general x2, matrix products, body(): lax.dot_general(basis, collision, (((1,), (1,)), ((), ())), precision=lax...  21.8 us
    dot_general x2, matrix products, body(): partial_energy = jnp.dot(fstar, basis[4], precision=lax.Precision.HIGHEST)  16.6 us
    sub x2, other arithmetic, advect(): return padded[2:length + 2] - (flux[1:] - flux[:-1])  9.98 us
  transfers between devices with their start and end apart: 4, of which 2 were waited for; matrix products, arithmetic and copies ran while one was open for 5% of the time, Pallas kernels for 0%

commit v1 on v0

v1 whole, which is shorter than its diff:
```python
import functools
import math

import jax
import jax.numpy as jnp
import numpy as np
from jax import lax
from jax.experimental import pallas as pl
from jax.experimental.pallas import tpu as pltpu
from jax.sharding import PartitionSpec as P

VGRID = 48
LATENT = 512
VBLOCKS = 96
STEPS = 2
VELS = 110592
WIDTH = VELS // VBLOCKS
LANES = 128
HALO = 4
SINK_RATE = 0.5
COURANT = 0.9
SCALE = math.sqrt(VELS / LATENT)
F32 = jnp.float32
BF16 = jnp.bfloat16


def grid_moments():
    centres = (2.0 * np.arange(VGRID) + 1.0 - VGRID) / VGRID
    second = float(np.sum(centres**2))
    fourth = float(np.sum(centres**4))
    number = float(VGRID)
    total = number**3
    cross = 3.0 * number * number * second
    quartic = 3.0 * number * number * fourth + 6.0 * number * second * second
    square = number * number * second
    return (total, cross, quartic, square)


def patterns():
    number = np.arange(WIDTH)
    rows = np.zeros((8, WIDTH), np.float32)
    for parity in range(2):
        rows[parity] = 2 * ((parity * WIDTH + number) // VGRID % VGRID) + 1 - VGRID
    rows[2] = 2 * (number % VGRID) + 1 - VGRID
    return rows


def taps(block):
    along = 2 * (block * WIDTH // (VGRID * VGRID)) + 1 - VGRID
    sign = jnp.where(along >= 0, 1, -1)
    along = along.astype(F32)
    a = jnp.abs(along) * (COURANT / VGRID)
    upwind = (1.0 - a) * 0.5
    curved = (1.0 - a * a) * (1.0 / 6.0)
    far = -a * curved
    behind = a * (1.0 - upwind + 3.0 * curved)
    here = 1.0 - a * (1.0 - 2.0 * upwind + 3.0 * curved)
    ahead = -a * (upwind - curved)
    return along, sign, (far, behind, here, ahead)


def stencil(ref, tile, first, count, sign, weights):
    far, behind, here, ahead = weights
    at = lambda shift: ref[tile, pl.ds(first + shift, count), :]
    return (
        far * at(-2 * sign) + behind * at(-sign) + here * at(0) + ahead * at(sign)
    )


def fill(pad, tile, lanes, density, left, right, inflow, open_left, open_right):
    cells = density.shape[0]
    ghost = inflow[:, lanes]
    pad[tile, 8 : 8 + cells, :] = density[:, lanes].astype(F32)
    pad[tile, 8 - HALO : 8, :] = jnp.where(open_left, left[:, lanes].astype(F32), ghost)
    pad[tile, 8 + cells : 8 + cells + HALO, :] = jnp.where(
        open_right, right[:, lanes].astype(F32), ghost
    )


def energy_row(total, rows):
    column = jnp.sum(total, axis=1, keepdims=True) * (1.0 / (VGRID * VGRID))
    row = lax.broadcasted_iota(jnp.int32, (rows, LANES), 0)
    lane = lax.broadcasted_iota(jnp.int32, (rows, LANES), 1)
    return jnp.sum(jnp.where(row == lane, column, 0.0), axis=0, keepdims=True)


def pattern_rows(pats, parity, lanes):
    y = jnp.where(parity == 0, pats[0:1, lanes], pats[1:2, lanes])
    return y, pats[2:3, lanes]


def first_kernel(
    nb, blocks, open_sides, density, left, right, inflow, coder, pats,
    sums, extra, pad, coarse, energy,
):
    step = pl.program_id(0)
    cells = density.shape[0]
    rows = cells + 2 * HALO
    tiles = WIDTH // LANES

    @pl.when(step == 0)
    def _():
        sums[...] = jnp.zeros_like(sums)
        energy[...] = jnp.zeros_like(energy)
        pad[...] = jnp.zeros_like(pad)

    open_left = open_sides[0] == 1
    open_right = open_sides[1] == 1
    kind = lax.broadcasted_iota(jnp.int32, (8, LANES), 0)
    for k in range(nb):
        block = blocks[step * nb + k]
        along, sign, weights = taps(block)
        parity = lax.rem(block, 2)
        total = energy[...]
        for t in range(tiles):
            lanes = slice(k * WIDTH + t * LANES, k * WIDTH + (t + 1) * LANES)
            tile = k * tiles + t
            fill(pad, tile, lanes, density, left, right, inflow, open_left, open_right)
            fstar = stencil(pad, tile, 8 - HALO, rows, sign, weights)
            y, z = pattern_rows(pats, parity, slice(t * LANES, (t + 1) * LANES))
            e = along * along + (y * y + z * z)
            total = total + fstar * e
            high = e.astype(BF16).astype(F32)
            basis = jnp.where(kind == 0, 1.0, 0.0)
            basis = jnp.where(kind == 1, along, basis)
            basis = jnp.where(kind == 2, y, basis)
            basis = jnp.where(kind == 3, z, basis)
            basis = jnp.where(kind == 4, high, basis)
            basis = jnp.where(kind == 5, e - high, basis)
            coarse[:, lanes] = jnp.concatenate([fstar, basis], 0).astype(BF16)
        energy[...] = total
    sums[...] += jnp.dot(coarse[...], coder[...], preferred_element_type=F32)

    @pl.when(step == pl.num_programs(0) - 1)
    def _():
        extra[0:1, :] = energy_row(energy[...], rows)


def prologue(active, moment_rows, energy, restitution, pats, consts, bands):
    total, cross, quartic, square = grid_moments()
    determinant = total * quartic - cross * cross
    rows = restitution.shape[0]
    inverse = 1.0 / VGRID
    act = active[0:rows, :].astype(F32)
    dots = [
        SCALE * jnp.sum(act * moment_rows[k : k + 1, :], axis=1, keepdims=True) for k in range(6)
    ]
    row = lax.broadcasted_iota(jnp.int32, (rows, LANES), 0)
    lane = lax.broadcasted_iota(jnp.int32, (rows, LANES), 1)
    energy_sum = jnp.sum(jnp.where(row == lane, energy[0:1, :], 0.0), axis=1, keepdims=True)
    r = restitution[...]
    sink = -SINK_RATE * (1.0 - r * r) * energy_sum
    excess = (dots[4] + dots[5]) * (inverse * inverse) - sink
    mass = (quartic * dots[0] - cross * excess) / determinant
    power = (total * excess - cross * dots[0]) / determinant * (inverse * inverse)
    slopes = [dots[k] * (inverse * inverse / square) for k in (1, 2, 3)]
    spread = lambda column: jnp.broadcast_to(column, (rows, LANES))
    consts[0] = spread(mass)
    consts[1] = spread(slopes[0])
    consts[2] = spread(power)
    power, second, third = spread(power), spread(slopes[1]), spread(slopes[2])
    for parity in range(2):
        for t in range(WIDTH // LANES):
            lanes = slice(t * LANES, (t + 1) * LANES)
            y, z = pats[parity : parity + 1, lanes], pats[2:3, lanes]
            bands[parity, t] = second * y + third * z + power * (y * y + z * z)


def second_kernel(
    nb, blocks, open_sides, density, left, right, inflow, coder, pats,
    active, moment_rows, energy_in, restitution,
    coarse, sums, extra, pad, state, decoded, energy, consts, bands,
):
    step = pl.program_id(0)
    cells = density.shape[0]
    rows = cells + 2 * HALO
    tiles = WIDTH // LANES

    @pl.when(step == 0)
    def _():
        sums[...] = jnp.zeros_like(sums)
        energy[...] = jnp.zeros_like(energy)
        pad[...] = jnp.zeros_like(pad)
        prologue(active, moment_rows, energy_in, restitution, pats, consts, bands)

    open_left = open_sides[0] == 1
    open_right = open_sides[1] == 1
    decoded[...] = lax.dot_general(
        active[...], coder[...], (((1,), (1,)), ((), ())), preferred_element_type=F32
    )
    for k in range(nb):
        block = blocks[step * nb + k]
        along, sign, weights = taps(block)
        parity = lax.rem(block, 2)
        level = consts[0] + along * consts[1] + (along * along) * consts[2]
        total = energy[...]
        for t in range(tiles):
            lanes = slice(k * WIDTH + t * LANES, k * WIDTH + (t + 1) * LANES)
            tile = k * tiles + t
            fill(pad, tile, lanes, density, left, right, inflow, open_left, open_right)
            fstar = stencil(pad, tile, 8 - HALO, rows, sign, weights)
            full = fstar + (SCALE * decoded[0:rows, lanes] - (level + bands[parity, t]))
            state[tile, :, :] = full
            ghost = jnp.broadcast_to(inflow[:, lanes], (HALO, LANES))

            @pl.when(jnp.logical_not(open_left))
            def _():
                state[tile, 0:HALO, :] = ghost

            @pl.when(jnp.logical_not(open_right))
            def _():
                state[tile, HALO + cells : rows, :] = ghost

            again = stencil(state, tile, HALO, cells, sign, weights)
            y, z = pattern_rows(pats, parity, slice(t * LANES, (t + 1) * LANES))
            total = total + again * (along * along + (y * y + z * z))
            coarse[:, lanes] = again.astype(BF16)
        energy[...] = total
    sums[...] += jnp.dot(coarse[...], coder[...], preferred_element_type=F32)

    @pl.when(step == pl.num_programs(0) - 1)
    def _():
        extra[0:1, :] = energy_row(energy[...], cells)


def third_kernel(
    nb, blocks, coarse, coder, pats, active, moment_rows, energy_in, restitution,
    out, decoded, consts, bands,
):
    step = pl.program_id(0)
    tiles = WIDTH // LANES

    @pl.when(step == 0)
    def _():
        prologue(active, moment_rows, energy_in, restitution, pats, consts, bands)

    decoded[...] = lax.dot_general(
        active[...], coder[...], (((1,), (1,)), ((), ())), preferred_element_type=F32
    )
    for k in range(nb):
        block = blocks[step * nb + k]
        along = (2 * (block * WIDTH // (VGRID * VGRID)) + 1 - VGRID).astype(F32)
        parity = lax.rem(block, 2)
        level = consts[0] + along * consts[1] + (along * along) * consts[2]
        for t in range(tiles):
            lanes = slice(k * WIDTH + t * LANES, k * WIDTH + (t + 1) * LANES)
            full = coarse[:, lanes].astype(F32) + (
                SCALE * decoded[:, lanes] - (level + bands[parity, t])
            )
            out[:, lanes] = full.astype(BF16)


def shifted(array, axes, count, shift):
    return lax.ppermute(array, axes, [(i, (i + shift) % count) for i in range(count)])


def latent_layer(encoded, w_latent, b_latent):
    mixed = jnp.dot(encoded.astype(BF16), w_latent, preferred_element_type=F32)
    return jnp.tanh(mixed + b_latent).astype(BF16)


def body(density, coder, w_latent, b_latent, restitution, inflow, flags, blocks):
    cells, vels = density.shape
    count = blocks.shape[0]
    nb = 2 if count % 2 == 0 else 1
    steps = count // nb
    tile = nb * WIDTH
    tiles = tile // LANES
    rows = cells + 2 * HALO
    ring = ("cell", "sub")
    sub_count = lax.axis_size("sub")
    ring_count = lax.axis_size("cell") * sub_count
    position = lax.axis_index("cell") * sub_count + lax.axis_index("sub")
    open_left = lax.dynamic_index_in_dim(flags, position, 0, keepdims=False)
    open_right = lax.dynamic_index_in_dim(flags, (position + 1) % ring_count, 0, keepdims=False)
    open_sides = jnp.stack([open_left, open_right])

    left = shifted(density[cells - HALO :], ring, ring_count, 1)
    right = shifted(density[:HALO], ring, ring_count, -1)
    left_r = shifted(restitution[cells - HALO :], ring, ring_count, 1)
    right_r = shifted(restitution[:HALO], ring, ring_count, -1)
    wide_r = jnp.concatenate([left_r, restitution, right_r])[:, None]
    pats = jnp.asarray(patterns())
    inflow = inflow[None, :]

    column = lambda height: pl.BlockSpec((height, tile), lambda i, *_: (0, i))
    whole = lambda *shape: pl.BlockSpec(shape, lambda i, *_: (0,) * len(shape))
    coder_spec = pl.BlockSpec((tile, LATENT), lambda i, *_: (i, 0))
    shape = jax.ShapeDtypeStruct
    params = pltpu.CompilerParams(
        dimension_semantics=("arbitrary",), vmem_limit_bytes=40 * 1024 * 1024
    )

    sums, extra = pl.pallas_call(
        functools.partial(first_kernel, nb),
        out_shape=(shape((rows + 8, LATENT), F32), shape((8, LANES), F32)),
        grid_spec=pltpu.PrefetchScalarGridSpec(
            num_scalar_prefetch=2,
            grid=(steps,),
            in_specs=[
                column(cells), column(HALO), column(HALO), column(1), coder_spec, whole(8, WIDTH),
            ],
            out_specs=(whole(rows + 8, LATENT), whole(8, LANES)),
            scratch_shapes=[
                pltpu.VMEM((tiles, rows + 8, LANES), F32),
                pltpu.VMEM((rows + 8, tile), BF16),
                pltpu.VMEM((rows, LANES), F32),
            ],
        ),
        compiler_params=params,
        name="first",
    )(blocks, open_sides, density, left, right, inflow, coder, pats)

    def exchange(sums, extra):
        sums, energy = lax.psum((sums, extra), "vel")
        return sums, energy

    sums, energy = exchange(sums, extra)
    moment_rows = sums[rows:]
    active = latent_layer(sums, w_latent, b_latent)

    coarse, sums, extra = pl.pallas_call(
        functools.partial(second_kernel, nb),
        out_shape=(
            shape((cells, vels), BF16), shape((cells, LATENT), F32), shape((8, LANES), F32),
        ),
        grid_spec=pltpu.PrefetchScalarGridSpec(
            num_scalar_prefetch=2,
            grid=(steps,),
            in_specs=[
                column(cells), column(HALO), column(HALO), column(1), coder_spec, whole(8, WIDTH),
                whole(rows + 8, LATENT), whole(8, LATENT), whole(8, LANES), whole(rows, 1),
            ],
            out_specs=(column(cells), whole(cells, LATENT), whole(8, LANES)),
            scratch_shapes=[
                pltpu.VMEM((tiles, rows + 8, LANES), F32),
                pltpu.VMEM((tiles, rows, LANES), F32),
                pltpu.VMEM((rows + 8, tile), F32),
                pltpu.VMEM((cells, LANES), F32),
                pltpu.VMEM((3, rows, LANES), F32),
                pltpu.VMEM((2, WIDTH // LANES, rows, LANES), F32),
            ],
        ),
        compiler_params=params,
        name="second",
    )(
        blocks, open_sides, density, left, right, inflow, coder, pats,
        active, moment_rows, energy, wide_r,
    )

    sums, energy = exchange(sums, extra)
    active = latent_layer(sums, w_latent, b_latent)

    return pl.pallas_call(
        functools.partial(third_kernel, nb),
        out_shape=shape((cells, vels), BF16),
        grid_spec=pltpu.PrefetchScalarGridSpec(
            num_scalar_prefetch=1,
            grid=(steps,),
            in_specs=[
                column(cells), coder_spec, whole(8, WIDTH),
                whole(cells, LATENT), whole(8, LATENT), whole(8, LANES), whole(cells, 1),
            ],
            out_specs=column(cells),
            scratch_shapes=[
                pltpu.VMEM((cells, tile), F32),
                pltpu.VMEM((3, cells, LANES), F32),
                pltpu.VMEM((2, WIDTH // LANES, cells, LANES), F32),
            ],
        ),
        compiler_params=params,
        name="third",
    )(blocks, coarse, coder, pats, active, moment_rows, energy, restitution[:, None])


def solution(mesh):
    return jax.shard_map(
        body,
        mesh=mesh,
        in_specs=(
            P(("groups", "cell", "sub"), "vel"),
            P("vel", None),
            P(),
            P(),
            P(("groups", "cell", "sub")),
            P(("groups", "vel")),
            P("groups"),
            P(("groups", "vel")),
        ),
        out_specs=P(("groups", "cell", "sub"), "vel"),
        check_vma=False,
    )
```

time: 269 us -> 169 us (0.63); the launches traced: 265 us -> 168 us
  matrix products: 130 us -> 1.4 us
  Pallas kernels: 0 us -> 71.5 us
  other arithmetic: 49.9 us -> 1.34 us
  blocking collectives: 62.6 us -> 33.4 us
  waiting for transfers between devices: 4.67 us -> 26.8 us
  between operations: 1.85 us -> 13.5 us
  local copies, waits for them, and re-layouts: 12.2 us -> 15.9 us
    dot_general x10 -> x2, matrix products: 130 us -> 1.4 us  [latent_layer(): mixed = jnp.dot(encoded.astype(BF16), w_latent, preferred_element_type=F32)]
    pallas_call x0 -> x3, Pallas kernels: none -> 71.5 us  [the longest x1 32.5 us: body(): pl.pallas_call(functools.partial(second_kernel, nb), out_shape=(shape((ce...]
    mul x3 -> x0, other arithmetic: 30 us -> none  [the longest x2 29.3 us: advect(): flux = courant * jnp.where(courant >= 0.0, forward, backward)]
    psum x4 -> x2, blocking collectives: 62.6 us -> 33.4 us  [exchange(): sums, energy = lax.psum((sums, extra), 'vel')]
    psum x0 -> x1, waiting for transfers between devices: none -> 21.3 us  [exchange(): sums, energy = lax.psum((sums, extra), 'vel')]
    sub x2 -> x0, other arithmetic: 9.98 us -> none  [advect(): return padded[2:length + 2] - (flux[1:] - flux[:-1])]
    convert_element_type x1 -> x0, other arithmetic: 7.47 us -> none  [body(): state = density.astype(jnp.float32)]
    unnamed x23 -> x26, local copies, waits for them, and re-layouts: 8.68 us -> 12.2 us
  transfers between devices with their start and end apart: 4 -> 5, of which waited for: 2 -> 4; matrix products, arithmetic and copies ran while one was open for 5% -> 2% of each run, Pallas kernels for 0% -> 0%
where the time goes in v1:
time: 169 us; the launch traced here: 168 us
  Pallas kernels  71.5 us (42%)
  blocking collectives  33.4 us (20%)
  waiting for transfers between devices  26.8 us (16%)
  local copies, waits for them, and re-layouts  15.9 us (9%)
  between operations  13.5 us (8%)
  starting transfers between devices  4.21 us (2%)
    psum x2, blocking collectives, exchange(): sums, energy = lax.psum((sums, extra), 'vel')  33.4 us
    pallas_call x1, Pallas kernels, body(): pl.pallas_call(functools.partial(second_kernel, nb), out_shape=(shape((ce...  32.5 us
    psum x1, waiting for transfers between devices, exchange(): sums, energy = lax.psum((sums, extra), 'vel')  21.3 us
    pallas_call x1, Pallas kernels, body(): pl.pallas_call(functools.partial(third_kernel, nb), out_shape=shape((cell...  19.6 us
    pallas_call x1, Pallas kernels, body(): pl.pallas_call(functools.partial(first_kernel, nb), out_shape=(shape((row...  19.4 us
    unnamed x26, local copies, waits for them, and re-layouts  12.2 us
    ppermute x4, waiting for transfers between devices, shifted(): lax.ppermute(array, axes, [(i, (i + shift) % count) for i in range(count)])  5.45 us
    ppermute x4, starting transfers between devices, shifted(): lax.ppermute(array, axes, [(i, (i + shift) % count) for i in range(count)])  4.2 us
  transfers between devices with their start and end apart: 5, of which 4 were waited for; matrix products, arithmetic and copies ran while one was open for 2% of the time, Pallas kernels for 0%

profile of v1, /device:TPU:0, one launch (start us, length us, event | category | flops | bytes accessed | tf_op | source)
XLA Modules:
  0.0 168.0 jit_solution(2027453192547915600)
XLA Ops:
  6.5 1.4 fusion.6
  7.9 2.5 %collective-permute-start.1 = (bf16[4,27648]{1,0:T(4,128)(2,1)S(1)}, bf16[4,27648]{1,0:T(4,128)(2,1)S(1)}, u32[]{:S(2)}, u32[]{:S(2)}) collective-permute-start(bf16[4,27648]{1,0:T(4,128)(2,1)S(1)} %get-tuple-element.17), channel_id=1, source_target_pairs={{0,3},{1,0},{2,1},{3,2},{4,7},{5,4},{6,5},{7,6},{8,11},{9,8},{10,9... | collective-permute-start | bytes 663560 | tf_op jit(solution)/shard_map/ppermute | solution.py:254
  10.4 1.3 fusion.8
  11.7 1.3 pad_add_fusion.open_sides
  13.0 3.2 %collective-permute-done.1.right = bf16[4,27648]{1,0:T(4,128)(2,1)S(1)} collective-permute-done((bf16[4,27648]{1,0:T(4,128)(2,1)S(1)}, bf16[4,27648]{1,0:T(4,128)(2,1)S(1)}, u32[]{:S(2)}, u32[]{:S(2)}) %collective-permute-start.1) | collective-permute-done | bytes 221216 | tf_op jit(solution)/shard_map/ppermute | solution.py:254
  16.1 1.1 collective-permute-done.left
  17.2 2.5 %copy-done.1 = bf16[96,27648]{1,0:T(8,128)(2,1)S(1)} copy-done((bf16[96,27648]{1,0:T(8,128)(2,1)S(1)}, bf16[96,27648]{1,0:T(8,128)(2,1)}, u32[]{:S(2)}) %copy-start.1) | copy-done | bytes 5308440
  19.7 0.9 copy-done.5
  20.6 0.8 copy-done.7
  21.4 0.7 copy-done.9
  22.1 19.4 %first.1 = (f32[112,512]{1,0:T(8,128)}, f32[8,128]{1,0:T(8,128)S(1)}) custom-call(s32[24]{0:T(128)S(1)} %copy-done.9, s32[2]{0:T(128)S(1)} %pad_add_fusion.open_sides, bf16[96,27648]{1,0:T(8,128)(2,1)S(1)} %copy-done.1, bf16[4,27648]{1,0:T(4,128)(2,1)S(1)} %collective-permute-done.left, bf16[4,27648]{1,0:T(4,128)(2,1)S(1)} %collective-permute-done.1.right, ...), custom_call_target="tpu_custom_call" | custom-call | tf_op jit(solution)/shard_map/first/pallas_call | solution.py:294
  41.5 0.0 all-reduce.4.cloned.1.call-update
  41.5 0.1 fusion.7
  41.6 1.7 %collective-permute-start.3 = (f32[4]{0:T(128)S(1)}, f32[4]{0:T(128)S(1)}, u32[]{:S(2)}, u32[]{:S(2)}) collective-permute-start(f32[4]{0:T(128)S(1)} %get-tuple-element.20), channel_id=1, source_target_pairs={{0,3},{1,0},{2,1},{3,2},{4,7},{5,4},{6,5},{7,6},{8,11},{9,8},{10,9... | collective-permute-start | bytes 56 | tf_op jit(solution)/shard_map/ppermute | solution.py:254
  43.3 0.1 copy.11.restitution
  43.4 1.1 collective-permute-done.2
  44.6 0.0 collective-permute-done.3
  44.6 0.1 maximum_bitcast_fusion
  44.7 0.1 copy.10.restitution
  44.8 12.0 %psum.29.energy_in = f32[8,128]{1,0:T(8,128)S(1)} all-reduce(f32[8,128]{1,0:T(8,128)S(1)} %get-tuple-element.11), channel_id=1, replica_groups=mesh['groups'=2,'vel'=4,'cell'=2,'sub'=2] {'vel'}, use_global_device_ids=true, to_apply=%region_1.2 | all-reduce | flops 1024 | bytes 8192 | tf_op jit(solution)/shard_map/psum | solution.py:315
  56.8 21.3 %all-reduce.4.cloned.1.call-done = f32[112,512]{1,0:T(8,128)} async-done(((f32[112,512]{1,0:T(8,128)}), f32[112,512]{1,0:T(8,128)}) %all-reduce.4.cloned.1.call-update) | async-done | bytes 229392 | tf_op jit(solution)/shard_map/psum | solution.py:315
  78.1 0.7 slice.20.moment_rows
  78.8 1.2 fusion.2.active
  80.0 0.0 copy-start.2
  80.0 2.5 %copy-done.2 = bf16[96,27648]{1,0:T(8,128)(2,1)S(1)} copy-done((bf16[96,27648]{1,0:T(8,128)(2,1)S(1)}, bf16[96,27648]{1,0:T(8,128)(2,1)}, u32[]{:S(2)}) %copy-start.2) | copy-done | bytes 5308440
  82.5 32.5 %second.1 = (bf16[96,27648]{1,0:T(8,128)(2,1)S(1)}, f32[96,512]{1,0:T(8,128)S(1)}, f32[8,128]{1,0:T(8,128)S(1)}) custom-call(s32[24]{0:T(128)S(1)} %copy-done.10, s32[2]{0:T(128)S(1)} %pad_add_fusion.open_sides, bf16[96,27648]{1,0:T(8,128)(2,1)S(1)} %copy-done.2, bf16[4,27648]{1,0:T(4,128)(2,1)S(1)} %collective-permute-done.left, ...), custom_call_target="tpu_custom_call" | custom-call | tf_op jit(solution)/shard_map/second/pallas_call | solution.py:322
  115.1 0.0 copy-start.3
  115.1 2.4 %copy-done.3 = bf16[96,27648]{1,0:T(8,128)(2,1)} copy-done((bf16[96,27648]{1,0:T(8,128)(2,1)}, bf16[96,27648]{1,0:T(8,128)(2,1)S(1)}, u32[]{:S(2)}) %copy-start.3) | copy-done | bytes 5308440
  117.4 21.4 %all-reduce.5 = (bf16[96,512]{1,0:T(8,128)(2,1)S(1)}, f32[8,128]{1,0:T(8,128)S(1)}) all-reduce(f32[96,512]{1,0:T(8,128)S(1)} %get-tuple-element.13, f32[8,128]{1,0:T(8,128)S(1)} %get-tuple-element.14), channel_id=1, replica_groups=mesh['groups'=2,'vel'=4,'cell'=2,'sub'=2] {'vel'}, use_global_device_ids=true, to_apply=%region_2.3 | all-reduce | flops 50176 | bytes 303104 | tf_op jit(solution)/shard_map/psum | solution.py:315
  138.8 0.2 fusion.3.active
  139.1 2.5 %copy-done.4 = bf16[96,27648]{1,0:T(8,128)(2,1)S(1)} copy-done((bf16[96,27648]{1,0:T(8,128)(2,1)S(1)}, bf16[96,27648]{1,0:T(8,128)(2,1)}, u32[]{:S(2)}) %copy-start.4) | copy-done | bytes 5308440
  141.6 19.6 %third.1 = bf16[96,27648]{1,0:T(8,128)(2,1)} custom-call(s32[24]{0:T(128)S(1)} %copy-done.10, bf16[96,27648]{1,0:T(8,128)(2,1)S(1)} %copy-done.4, bf16[27648,512]{1,0:T(8,128)(2,1)} %coder.5, f32[8,1152]{1,0:T(8,128)S(1)} %copy-done.8, bf16[96,512]{1,0:T(8,128)(2,1)S(1)} %fusion.3.active, f32[8,512]{1,0:T(8,128)S(1)} %slice.20.moment_rows, ...), custom_call_target="tpu_custom_call" | custom-call | tf_op jit(solution)/shard_map/third/pallas_call | solution.py:354
  (20 shorter events, 0.0 us)
Async XLA Ops:
  6.5 72.3 %copy-start = (bf16[512,512]{1,0:T(8,128)(2,1)S(1)}, bf16[512,512]{1,0:T(8,128)(2,1)}, u32[]{:S(2)}) copy-start(bf16[512,512]{1,0:T(8,128)(2,1)} %param.11) | copy-start | bytes 1572868
  6.5 71.5 %all-reduce.4.cloned.1.call-start = ((), (), s32[]{:S(2)}) async-start(), calls=%async_computation | async-start | bytes 458752 | tf_op jit(solution)/shard_map/psum | solution.py:315
  7.9 8.2 %collective-permute-start.1 = (bf16[4,27648]{1,0:T(4,128)(2,1)S(1)}, bf16[4,27648]{1,0:T(4,128)(2,1)S(1)}, u32[]{:S(2)}, u32[]{:S(2)}) collective-permute-start(bf16[4,27648]{1,0:T(4,128)(2,1)S(1)} %get-tuple-element.17), channel_id=1, source_target_pairs={{0,3},{1,0},{2,1},{3,2},{4,7},{5,4},{6,5},{7,6},{8,11},{9,8},{10,9... | collective-permute-start | bytes 663560 | tf_op jit(solution)/shard_map/ppermute | solution.py:254
  10.4 6.8 %collective-permute-start = (bf16[4,27648]{1,0:T(4,128)(2,1)S(1)}, bf16[4,27648]{1,0:T(4,128)(2,1)S(1)}, u32[]{:S(2)}, u32[]{:S(2)}) collective-permute-start(bf16[4,27648]{1,0:T(4,128)(2,1)S(1)} %get-tuple-element.18), channel_id=1, source_target_pairs={{0,1},{1,2},{2,3},{3,0},{4,5},{5,6},{6,7},{7,4},{8,9},{9,10},{10,1... | collective-permute-start | bytes 663560 | tf_op jit(solution)/shard_map/ppermute | solution.py:254
  17.2 2.5 %copy-start.1 = (bf16[96,27648]{1,0:T(8,128)(2,1)S(1)}, bf16[96,27648]{1,0:T(8,128)(2,1)}, u32[]{:S(2)}) copy-start(bf16[96,27648]{1,0:T(8,128)(2,1)} %density.3) | copy-start | bytes 15925252
  19.7 0.9 copy-start.5
  20.6 0.8 copy-start.7
  21.4 0.7 copy-start.9
  22.0 19.5 %copy-start.12 = (f32[96]{0:T(128)S(1)}, f32[96]{0:T(128)}, u32[]{:S(2)}) copy-start(f32[96]{0:T(128)} %param.13) | copy-start | bytes 1156
  22.1 56.8 %copy-start.11 = (f32[512]{0:T(512)S(1)}, f32[512]{0:T(512)}, u32[]{:S(2)}) copy-start(f32[512]{0:T(512)} %param.12) | copy-start | bytes 6148
  22.1 57.9 %copy-start.6 = (f32[27648]{0:T(1024)S(1)}, f32[27648]{0:T(1024)}, u32[]{:S(2)}) copy-start(f32[27648]{0:T(1024)} %param.14) | copy-start | bytes 331780
  22.1 57.9 %copy-start.8 = (f32[8,1152]{1,0:T(8,128)S(1)}, f32[8,1152]{1,0:T(8,128)}, u32[]{:S(2)}) copy-start(f32[8,1152]{1,0:T(8,128)} %constant.31.clone.pats) | copy-start | bytes 110596
  22.1 57.9 %copy-start.10 = (s32[24]{0:T(128)S(1)}, s32[24]{0:T(128)}, u32[]{:S(2)}) copy-start(s32[24]{0:T(128)} %blocks.5) | copy-start | bytes 292
  41.6 3.0 %collective-permute-start.2 = (f32[4]{0:T(128)S(1)}, f32[4]{0:T(128)S(1)}, u32[]{:S(2)}, u32[]{:S(2)}) collective-permute-start(f32[4]{0:T(128)S(1)} %get-tuple-element.19), channel_id=1, source_target_pairs={{0,1},{1,2},{2,3},{3,0},{4,5},{5,6},{6,7},{7,4},{8,9},{9,10},{10,1... | collective-permute-start | bytes 56 | tf_op jit(solution)/shard_map/ppermute | solution.py:254
  41.6 3.0 %collective-permute-start.3 = (f32[4]{0:T(128)S(1)}, f32[4]{0:T(128)S(1)}, u32[]{:S(2)}, u32[]{:S(2)}) collective-permute-start(f32[4]{0:T(128)S(1)} %get-tuple-element.20), channel_id=1, source_target_pairs={{0,3},{1,0},{2,1},{3,2},{4,7},{5,4},{6,5},{7,6},{8,11},{9,8},{10,9... | collective-permute-start | bytes 56 | tf_op jit(solution)/shard_map/ppermute | solution.py:254
  80.0 2.5 %copy-start.2 = (bf16[96,27648]{1,0:T(8,128)(2,1)S(1)}, bf16[96,27648]{1,0:T(8,128)(2,1)}, u32[]{:S(2)}) copy-start(bf16[96,27648]{1,0:T(8,128)(2,1)} %density.3) | copy-start | bytes 15925252
  115.1 2.4 %copy-start.3 = (bf16[96,27648]{1,0:T(8,128)(2,1)}, bf16[96,27648]{1,0:T(8,128)(2,1)S(1)}, u32[]{:S(2)}) copy-start(bf16[96,27648]{1,0:T(8,128)(2,1)S(1)} %get-tuple-element.12.coarse) | copy-start | bytes 15925252
  139.1 2.5 %copy-start.4 = (bf16[96,27648]{1,0:T(8,128)(2,1)S(1)}, bf16[96,27648]{1,0:T(8,128)(2,1)}, u32[]{:S(2)}) copy-start(bf16[96,27648]{1,0:T(8,128)(2,1)} %copy-done.3) | copy-start | bytes 15925252
Sparse Core Ops, SparseCore 0:
  41.6 36.4 all-reduce.3

commit v2 on v0

v2 whole, which is shorter than its diff:
```python
import functools
import math

import jax
import jax.numpy as jnp
import numpy as np
from jax import lax
from jax.experimental import pallas as pl
from jax.experimental.pallas import tpu as pltpu
from jax.sharding import PartitionSpec as P

VGRID = 48
LATENT = 512
VBLOCKS = 96
STEPS = 2
VELS = 110592
WIDTH = VELS // VBLOCKS
LANES = 128
HALO = 4
SINK_RATE = 0.5
COURANT = 0.9
SCALE = math.sqrt(VELS / LATENT)
F32 = jnp.float32
BF16 = jnp.bfloat16


def grid_moments():
    centres = (2.0 * np.arange(VGRID) + 1.0 - VGRID) / VGRID
    second = float(np.sum(centres**2))
    fourth = float(np.sum(centres**4))
    number = float(VGRID)
    total = number**3
    cross = 3.0 * number * number * second
    quartic = 3.0 * number * number * fourth + 6.0 * number * second * second
    square = number * number * second
    return (total, cross, quartic, square)


def moment_pattern(pats):
    number = lax.broadcasted_iota(jnp.int32, (1, WIDTH), 1).astype(F32)
    along_y = jnp.floor((number + 0.5) * (1.0 / VGRID))
    along_z = number - VGRID * along_y
    first = 2.0 * along_y + (1 - VGRID)
    pats[0:1, :] = first
    pats[1:2, :] = first + (2 * WIDTH // VGRID)
    pats[2:3, :] = 2.0 * along_z + (1 - VGRID)


def taps(block):
    along = 2 * (block * WIDTH // (VGRID * VGRID)) + 1 - VGRID
    sign = jnp.where(along >= 0, 1, -1)
    along = along.astype(F32)
    a = jnp.abs(along) * (COURANT / VGRID)
    upwind = (1.0 - a) * 0.5
    curved = (1.0 - a * a) * (1.0 / 6.0)
    far = -a * curved
    behind = a * (1.0 - upwind + 3.0 * curved)
    here = 1.0 - a * (1.0 - 2.0 * upwind + 3.0 * curved)
    ahead = -a * (upwind - curved)
    return along, sign, (far, behind, here, ahead)


def stencil(ref, tile, first, count, sign, weights):
    far, behind, here, ahead = weights
    at = lambda shift: ref[tile, pl.ds(first + shift, count), :]
    return (
        far * at(-2 * sign) + behind * at(-sign) + here * at(0) + ahead * at(sign)
    )


def fill(pad, tile, lanes, far_lanes, density, left, right, inflow, open_left, open_right):
    cells = density.shape[0]
    ghost = inflow[:, far_lanes]
    pad[tile, 8 : 8 + cells, :] = density[:, lanes].astype(F32)
    pad[tile, 8 - HALO : 8, :] = jnp.where(open_left, left[:, far_lanes].astype(F32), ghost)
    pad[tile, 8 + cells : 8 + cells + HALO, :] = jnp.where(
        open_right, right[:, far_lanes].astype(F32), ghost
    )


def energy_row(total, rows):
    column = jnp.sum(total, axis=1, keepdims=True) * (1.0 / (VGRID * VGRID))
    row = lax.broadcasted_iota(jnp.int32, (rows, LANES), 0)
    lane = lax.broadcasted_iota(jnp.int32, (rows, LANES), 1)
    return jnp.sum(jnp.where(row == lane, column, 0.0), axis=0, keepdims=True)


def pattern_rows(pats, parity, lanes):
    y = jnp.where(parity == 0, pats[0:1, lanes], pats[1:2, lanes])
    return y, pats[2:3, lanes]


def sides(flags):
    sub_count = lax.axis_size("sub")
    count = lax.axis_size("cell") * sub_count
    position = lax.axis_index("cell") * sub_count + lax.axis_index("sub")
    return flags[position] == 1, flags[lax.rem(position + 1, count)] == 1


class Stream:
    def __init__(self, source, buffers, sems, tile, axis, inward=True):
        self.source, self.buffers, self.sems = source, buffers, sems
        self.tile, self.axis, self.inward = tile, axis, inward
        self.count = source.shape[axis] // tile
        self.slots = buffers.shape[0]

    def copy(self, i):
        slot = lax.rem(i, self.slots)
        span = pl.ds(pl.multiple_of(i * self.tile, LANES), self.tile)
        far = self.source.at[span, :] if self.axis == 0 else self.source.at[:, span]
        near = self.buffers.at[slot]
        source, target = (far, near) if self.inward else (near, far)
        return pltpu.make_async_copy(source, target, self.sems.at[slot])

    def begin(self, ahead):
        for i in range(min(ahead, self.count)):
            self.copy(i).start()

    def start(self, i):
        if isinstance(i, int):
            if i < self.count:
                self.copy(i).start()
        else:

            @pl.when(i < self.count)
            def _():
                self.copy(i).start()

    def wait(self, i):
        self.copy(i).wait()

    def at(self, i):
        return self.buffers.at[lax.rem(i, self.slots)]


def paired(first, last, step):
    pairs = (last - first) // 2
    if pairs > 1:

        def trip(j, carry):
            step(first + 2 * j, first % 2)
            step(first + 2 * j + 1, (first + 1) % 2)
            return carry

        lax.fori_loop(0, pairs, trip, 0)
        first = first + 2 * pairs
    for i in range(first, last):
        step(i, i % 2)


def scatter_rows(messages, sums, chunk, extra):
    count = len(messages)
    me = lax.axis_index("vel")
    for s in range(count):
        for k in range(count):

            @pl.when(lax.rem(me + s, count) == k)
            def _():
                messages[s][0:chunk, :] = sums[k * chunk : (k + 1) * chunk, :]

        for row, value in extra:
            messages[s][row : row + value.shape[0], 0 : value.shape[1]] = value


def gather_rows(wide, parts, chunk):
    count = len(parts)
    me = lax.axis_index("vel")
    for s in range(count):
        for k in range(count):

            @pl.when(lax.rem(me - s + count, count) == k)
            def _():
                wide[k * chunk : (k + 1) * chunk, :] = parts[s][0:chunk, :].astype(F32)


def first_kernel(shards, nb, blocks, flags, density, left, right, inflow, coder, *refs):
    messages = refs[:shards]
    pad, coarse_a, coarse_b, energy, pats, sums, tiles_c, sem_c, tiles_d, sem_d = refs[shards:]
    cells = density.shape[0]
    rows = cells + 2 * HALO
    width = nb * WIDTH
    tiles = WIDTH // LANES
    coders = Stream(coder, tiles_c, sem_c, width, 0)
    cells_in = Stream(density, tiles_d, sem_d, width, 1)
    ahead_c, ahead_d = coders.slots - 1, cells_in.slots
    coders.begin(ahead_c)
    cells_in.begin(ahead_d)
    steps = coders.count
    coarse = (coarse_a, coarse_b)

    moment_pattern(pats)
    sums[...] = jnp.zeros_like(sums)
    energy[...] = jnp.zeros_like(energy)
    pad[...] = jnp.zeros_like(pad)
    open_left, open_right = sides(flags)
    kind = lax.broadcasted_iota(jnp.int32, (8, LANES), 0)

    def transport(i, par):
        source = cells_in.at(i)
        for k in range(nb):
            block = blocks[i * nb + k]
            along, sign, weights = taps(block)
            parity = lax.rem(block, 2)
            total = energy[...]
            for t in range(tiles):
                tile = k * tiles + t
                lanes = slice(tile * LANES, (tile + 1) * LANES)
                far = pl.ds(pl.multiple_of(i * width + tile * LANES, LANES), LANES)
                fill(pad, tile, lanes, far, source, left, right, inflow, open_left, open_right)
                fstar = stencil(pad, tile, 8 - HALO, rows, sign, weights)
                y, z = pattern_rows(pats, parity, slice(t * LANES, (t + 1) * LANES))
                e = along * along + (y * y + z * z)
                total = total + fstar * e
                high = e.astype(BF16).astype(F32)
                basis = jnp.where(kind == 0, 1.0, 0.0)
                basis = jnp.where(kind == 1, along, basis)
                basis = jnp.where(kind == 2, y, basis)
                basis = jnp.where(kind == 3, z, basis)
                basis = jnp.where(kind == 4, high, basis)
                basis = jnp.where(kind == 5, e - high, basis)
                coarse[par][:, lanes] = jnp.concatenate([fstar, basis], 0).astype(BF16)
            energy[...] = total

    def encode(i, par):
        sums[...] += jnp.dot(coarse[par][...], coders.at(i)[...], preferred_element_type=F32)

    def step(i, par):
        cells_in.wait(i)
        coders.wait(i)
        coders.start(i + ahead_c - 1)
        encode(i - 1, 1 - par)
        transport(i, par)
        cells_in.start(i + ahead_d)

    cells_in.wait(0)
    transport(0, 0)
    cells_in.start(ahead_d)
    coders.wait(0)
    paired(1, steps, step)
    encode(steps - 1, (steps - 1) % 2)

    moments = sums[rows : rows + 4, :]
    last = sums[rows + 4 : rows + 5, :] + sums[rows + 5 : rows + 6, :]
    chunk = rows // shards
    scatter_rows(
        messages, sums, chunk,
        ((chunk, moments), (chunk + 4, last), (chunk + 5, energy_row(energy[...], rows))),
    )


def project(act, moments, energy, restitution, pats, consts, bands):
    total, cross, quartic, square = grid_moments()
    determinant = total * quartic - cross * cross
    rows = restitution.shape[0]
    inverse = 1.0 / VGRID
    dots = [
        SCALE * jnp.sum(act * moments[k : k + 1, :], axis=1, keepdims=True) for k in range(5)
    ]
    row = lax.broadcasted_iota(jnp.int32, (rows, LANES), 0)
    lane = lax.broadcasted_iota(jnp.int32, (rows, LANES), 1)
    energy_sum = jnp.sum(jnp.where(row == lane, energy, 0.0), axis=1, keepdims=True)
    sink = -SINK_RATE * (1.0 - restitution * restitution) * energy_sum
    excess = dots[4] * (inverse * inverse) - sink
    mass = (quartic * dots[0] - cross * excess) / determinant
    power = (total * excess - cross * dots[0]) / determinant * (inverse * inverse)
    slopes = [dots[k] * (inverse * inverse / square) for k in (1, 2, 3)]
    spread = lambda column: jnp.broadcast_to(column, (rows, LANES))
    consts[0] = spread(mass)
    consts[1] = spread(slopes[0])
    consts[2] = spread(power)
    power, second, third = spread(power), spread(slopes[1]), spread(slopes[2])
    for parity in range(2):
        for t in range(WIDTH // LANES):
            lanes = slice(t * LANES, (t + 1) * LANES)
            y, z = pats[parity : parity + 1, lanes], pats[2:3, lanes]
            bands[parity, t] = second * y + third * z + power * (y * y + z * z)


def diagonal(row, first, rows):
    shape = (rows, row.shape[1])
    place = lax.broadcasted_iota(jnp.int32, shape, 0) - first
    lane = lax.broadcasted_iota(jnp.int32, shape, 1)
    return jnp.sum(jnp.where(place == lane, row, 0.0), axis=1, keepdims=True)


def second_kernel(
    shards, nb, blocks, flags, density, left, right, inflow, coder, mine, restitution, *refs
):
    parts, refs = refs[:shards], refs[shards:]
    out, messages, refs = refs[0], refs[1 : 1 + shards], refs[1 + shards :]
    (
        pad, state, decoded_a, decoded_b, coarse, energy, pats, sums, wide, active, consts, bands,
        tiles_c, sem_c, tiles_d, sem_d, sem_o,
    ) = refs
    cells = density.shape[0]
    rows = cells + 2 * HALO
    width = nb * WIDTH
    tiles = WIDTH // LANES
    coders = Stream(coder, tiles_c, sem_c, width, 0)
    cells_in = Stream(density, tiles_d, sem_d, width, 1)
    cells_out = Stream(out, coarse, sem_o, width, 1, inward=False)
    ahead_c, ahead_d = coders.slots - 2, cells_in.slots
    coders.begin(ahead_c)
    cells_in.begin(ahead_d)
    steps = coders.count
    decoded = (decoded_a, decoded_b)
    vels = density.shape[1]

    moment_pattern(pats)
    sums[...] = jnp.zeros_like(sums)
    energy[...] = jnp.zeros_like(energy)
    pad[...] = jnp.zeros_like(pad)
    open_left, open_right = sides(flags)
    chunk = rows // shards
    gather_rows(wide, parts, chunk)
    active[...] = jnp.zeros_like(active)
    active[0:rows, :] = wide[...].astype(BF16)
    ghosts = [jnp.sum(side[:, vels:].astype(F32), axis=1, keepdims=True) for side in (left, right)]
    r = diagonal(restitution[...], HALO, rows)
    state[0, 0:rows, :] = jnp.broadcast_to(r, (rows, LANES))
    state[0, 0:HALO, :] = jnp.broadcast_to(ghosts[0], (HALO, LANES))
    state[0, HALO + cells : rows, :] = jnp.broadcast_to(ghosts[1], (HALO, LANES))
    project(
        wide[...], mine[chunk : chunk + 5, :], mine[chunk + 5 : chunk + 6, 0:LANES],
        state[0, :, 0:1], pats, consts, bands,
    )
    place = lax.broadcasted_iota(jnp.int32, (8, LANES), 0)
    cut_top = jnp.logical_and(place < HALO, jnp.logical_not(open_left))
    cut_bottom = jnp.logical_and(place >= 8 - HALO, jnp.logical_not(open_right))

    def decode(i, par):
        decoded[par][...] = lax.dot_general(
            active[...], coders.at(i)[...], (((1,), (1,)), ((), ())), preferred_element_type=F32
        )

    def transport(i, par):
        source = cells_in.at(i)
        target = cells_out.at(i)
        for k in range(nb):
            block = blocks[i * nb + k]
            along, sign, weights = taps(block)
            parity = lax.rem(block, 2)
            level = consts[0] + along * consts[1] + (along * along) * consts[2]
            total = energy[...]
            for t in range(tiles):
                tile = k * tiles + t
                lanes = slice(tile * LANES, (tile + 1) * LANES)
                far = pl.ds(pl.multiple_of(i * width + tile * LANES, LANES), LANES)
                fill(pad, tile, lanes, far, source, left, right, inflow, open_left, open_right)
                fstar = stencil(pad, tile, 8 - HALO, rows, sign, weights)
                full = fstar + (
                    SCALE * decoded[par][0:rows, lanes] - (level + bands[parity, t])
                )
                ghost = inflow[:, far]
                state[tile, 0:8, :] = jnp.where(cut_top, ghost, full[0:8])
                state[tile, 8 : rows - 8, :] = full[8 : rows - 8]
                state[tile, rows - 8 : rows, :] = jnp.where(cut_bottom, ghost, full[rows - 8 :])
                again = stencil(state, tile, HALO, cells, sign, weights)
                y, z = pattern_rows(pats, parity, slice(t * LANES, (t + 1) * LANES))
                total = total + again * (along * along + (y * y + z * z))
                target[:, lanes] = again.astype(BF16)
            energy[...] = total

    def encode(i, par):
        sums[...] += jnp.dot(
            cells_out.at(i)[...], coders.at(i)[...], preferred_element_type=F32
        )

    def step(i, par):
        cells_in.wait(i)
        coders.wait(i + 1)
        coders.start(i + ahead_c)
        if isinstance(i, int):
            if i >= cells_out.slots:
                cells_out.wait(i - cells_out.slots)
        else:

            @pl.when(i >= cells_out.slots)
            def _():
                cells_out.wait(i - cells_out.slots)

        encode(i - 1, 1 - par)
        decode(i + 1, 1 - par)
        transport(i, par)
        cells_in.start(i + ahead_d)
        cells_out.start(i)

    coders.wait(0)
    decode(0, 0)
    cells_in.wait(0)
    coders.wait(1)
    coders.start(ahead_c)
    decode(1, 1)
    transport(0, 0)
    cells_in.start(ahead_d)
    cells_out.start(0)
    paired(1, steps - 1, step)
    last = steps - 1
    cells_in.wait(last)
    if last >= cells_out.slots:
        cells_out.wait(last - cells_out.slots)
    encode(last - 1, (last - 1) % 2)
    transport(last, last % 2)
    cells_out.start(last)
    encode(last, last % 2)
    chunk = cells // shards
    scatter_rows(messages, sums, chunk, ((rows // shards + 5, energy_row(energy[...], cells)),))
    for i in range(max(0, steps - cells_out.slots), steps):
        cells_out.wait(i)


def third_kernel(shards, nb, blocks, source, coder, mine, energies, restitution, *refs):
    parts, refs = refs[:shards], refs[shards:]
    (
        out, decoded_a, decoded_b, result, pats, wide, active, consts, bands,
        tiles_c, sem_c, tiles_d, sem_d, sem_o,
    ) = refs
    cells = source.shape[0]
    rows = cells + 2 * HALO
    width = nb * WIDTH
    tiles = WIDTH // LANES
    coders = Stream(coder, tiles_c, sem_c, width, 0)
    cells_in = Stream(source, tiles_d, sem_d, width, 1)
    cells_out = Stream(out, result, sem_o, width, 1, inward=False)
    ahead_c, ahead_d = coders.slots - 1, cells_in.slots
    coders.begin(ahead_c)
    cells_in.begin(ahead_d)
    steps = coders.count
    decoded = (decoded_a, decoded_b)

    moment_pattern(pats)
    gather_rows(wide, parts, cells // shards)
    active[...] = wide[...].astype(BF16)
    chunk = rows // shards
    project(
        wide[...], mine[chunk : chunk + 5, :], energies[chunk + 5 : chunk + 6, 0:LANES],
        diagonal(restitution[...], 0, cells), pats, consts, bands,
    )

    def decode(i, par):
        decoded[par][...] = lax.dot_general(
            active[...], coders.at(i)[...], (((1,), (1,)), ((), ())), preferred_element_type=F32
        )

    def finish(i, par):
        here = cells_in.at(i)
        target = cells_out.at(i)
        for k in range(nb):
            block = blocks[i * nb + k]
            along = (2 * (block * WIDTH // (VGRID * VGRID)) + 1 - VGRID).astype(F32)
            parity = lax.rem(block, 2)
            level = consts[0] + along * consts[1] + (along * along) * consts[2]
            for t in range(tiles):
                tile = k * tiles + t
                lanes = slice(tile * LANES, (tile + 1) * LANES)
                full = here[:, lanes].astype(F32) + (
                    SCALE * decoded[par][:, lanes] - (level + bands[parity, t])
                )
                target[:, lanes] = full.astype(BF16)

    def drain(i):
        if isinstance(i, int):
            if i >= cells_out.slots:
                cells_out.wait(i - cells_out.slots)
        else:

            @pl.when(i >= cells_out.slots)
            def _():
                cells_out.wait(i - cells_out.slots)

    def step(i, par):
        coders.wait(i)
        coders.start(i + ahead_c)
        cells_in.wait(i - 1)
        drain(i - 1)
        decode(i, par)
        finish(i - 1, 1 - par)
        cells_in.start(i - 1 + ahead_d)
        cells_out.start(i - 1)

    coders.wait(0)
    coders.start(ahead_c)
    decode(0, 0)
    paired(1, steps, step)
    last = steps - 1
    cells_in.wait(last)
    drain(last)
    finish(last, last % 2)
    cells_out.start(last)
    for i in range(max(0, steps - cells_out.slots), steps):
        cells_out.wait(i)


def shifted(array, axes, count, shift):
    return lax.ppermute(array, axes, [(i, (i + shift) % count) for i in range(count)])


def latent_layer(encoded, w_latent, b_latent):
    mixed = jnp.dot(encoded.astype(BF16), w_latent, preferred_element_type=F32)
    return jnp.tanh(mixed + b_latent).astype(BF16)


def pieces(values):
    first = lax.reduce_precision(values, 8, 7)
    second = lax.reduce_precision(values - first, 8, 7)
    third = values - first - second
    return jnp.stack([first, second, third], -1).astype(BF16)


def exchange(messages, w_latent, b_latent):
    count = len(messages)
    total = messages[0] if count > 1 else lax.psum(messages[0], "vel")
    for s in range(1, count):
        total = total + shifted(messages[s], "vel", count, s)
    own = latent_layer(total, w_latent, b_latent)
    return total, [own] + [shifted(own, "vel", count, s) for s in range(1, count)]


def body(density, coder, w_latent, b_latent, restitution, inflow, flags, blocks):
    cells, vels = density.shape
    count = blocks.shape[0]
    nb = 2 if count % 2 == 0 else 1
    width = nb * WIDTH
    tiles = width // LANES
    rows = cells + 2 * HALO
    ring = ("cell", "sub")
    ring_count = lax.axis_size("cell") * lax.axis_size("sub")
    shards = lax.axis_size("vel")
    if rows % shards or cells % shards or shards > 8:
        shards = 1

    def edge(part, r):
        extra = jnp.pad(pieces(r), ((0, 0), (0, LANES - 3)))
        return jnp.concatenate([part, extra], 1)

    left = shifted(edge(density[cells - HALO :], restitution[cells - HALO :]), ring, ring_count, 1)
    right = shifted(edge(density[:HALO], restitution[:HALO]), ring, ring_count, -1)
    inflow = inflow[None, :]
    restitution = restitution[None, :]

    shape = jax.ShapeDtypeStruct
    vmem = pl.BlockSpec(memory_space=pltpu.VMEM)
    smem = pl.BlockSpec(memory_space=pltpu.SMEM)
    hbm = pl.BlockSpec(memory_space=pl.ANY)
    params = pltpu.CompilerParams(vmem_limit_bytes=60 * 1024 * 1024)
    dma = pltpu.SemaphoreType.DMA
    message = shape((-(-(rows // shards + 6) // 8) * 8, LATENT), F32)

    messages = pl.pallas_call(
        functools.partial(first_kernel, shards, nb),
        out_shape=(message,) * shards,
        in_specs=[smem, smem, hbm, vmem, vmem, vmem, hbm],
        out_specs=(vmem,) * shards,
        scratch_shapes=[
            pltpu.VMEM((tiles, rows + 8, LANES), F32),
            pltpu.VMEM((rows + 8, width), BF16),
            pltpu.VMEM((rows + 8, width), BF16),
            pltpu.VMEM((rows, LANES), F32),
            pltpu.VMEM((8, WIDTH), F32),
            pltpu.VMEM((rows + 8, LATENT), F32),
            pltpu.VMEM((5, width, LATENT), BF16),
            dma((5,)),
            pltpu.VMEM((3, cells, width), BF16),
            dma((3,)),
        ],
        compiler_params=params,
        name="first",
    )(blocks, flags, density, left, right, inflow, coder)

    mine, parts = exchange(messages, w_latent, b_latent)

    coarse, *messages = pl.pallas_call(
        functools.partial(second_kernel, shards, nb),
        out_shape=(shape((cells, vels), BF16),) + (message,) * shards,
        in_specs=[smem, smem, hbm, vmem, vmem, vmem, hbm, vmem, vmem] + [vmem] * shards,
        out_specs=(hbm,) + (vmem,) * shards,
        scratch_shapes=[
            pltpu.VMEM((tiles, rows + 8, LANES), F32),
            pltpu.VMEM((tiles, rows, LANES), F32),
            pltpu.VMEM((rows + 8, width), F32),
            pltpu.VMEM((rows + 8, width), F32),
            pltpu.VMEM((2, cells, width), BF16),
            pltpu.VMEM((cells, LANES), F32),
            pltpu.VMEM((8, WIDTH), F32),
            pltpu.VMEM((cells, LATENT), F32),
            pltpu.VMEM((rows, LATENT), F32),
            pltpu.VMEM((rows + 8, LATENT), BF16),
            pltpu.VMEM((3, rows, LANES), F32),
            pltpu.VMEM((2, WIDTH // LANES, rows, LANES), F32),
            pltpu.VMEM((6, width, LATENT), BF16),
            dma((6,)),
            pltpu.VMEM((3, cells, width), BF16),
            dma((3,)),
            dma((2,)),
        ],
        compiler_params=params,
        name="second",
    )(blocks, flags, density, left, right, inflow, coder, mine, restitution, *parts)

    energies, parts = exchange(messages, w_latent, b_latent)

    return pl.pallas_call(
        functools.partial(third_kernel, shards, nb),
        out_shape=shape((cells, vels), BF16),
        in_specs=[smem, hbm, hbm, vmem, vmem, vmem] + [vmem] * shards,
        out_specs=hbm,
        scratch_shapes=[
            pltpu.VMEM((cells, width), F32),
            pltpu.VMEM((cells, width), F32),
            pltpu.VMEM((2, cells, width), BF16),
            pltpu.VMEM((8, WIDTH), F32),
            pltpu.VMEM((cells, LATENT), F32),
            pltpu.VMEM((cells, LATENT), BF16),
            pltpu.VMEM((3, cells, LANES), F32),
            pltpu.VMEM((2, WIDTH // LANES, cells, LANES), F32),
            pltpu.VMEM((5, width, LATENT), BF16),
            dma((5,)),
            pltpu.VMEM((3, cells, width), BF16),
            dma((3,)),
            dma((2,)),
        ],
        compiler_params=params,
        name="third",
    )(blocks, coarse, coder, mine, energies, restitution, *parts)


def solution(mesh):
    return jax.shard_map(
        body,
        mesh=mesh,
        in_specs=(
            P(("groups", "cell", "sub"), "vel"),
            P("vel", None),
            P(),
            P(),
            P(("groups", "cell", "sub")),
            P(("groups", "vel")),
            P("groups"),
            P(("groups", "vel")),
        ),
        out_specs=P(("groups", "cell", "sub"), "vel"),
        check_vma=False,
    )
```

time: 269 us -> 115 us (0.43); the launches traced: 265 us -> 115 us
  matrix products: 130 us -> 0.41 us
  Pallas kernels: 0 us -> 64.8 us
  blocking collectives: 62.6 us -> 0 us
  other arithmetic: 49.9 us -> 2.89 us
  waiting for transfers between devices: 4.67 us -> 23.9 us
  starting transfers between devices: 4.32 us -> 19 us
  local copies, waits for them, and re-layouts: 12.2 us -> 3.87 us
    dot_general x10 -> x2, matrix products: 130 us -> 0.41 us  [latent_layer(): mixed = jnp.dot(encoded.astype(BF16), w_latent, preferred_element_type=F32)]
    pallas_call x0 -> x3, Pallas kernels: none -> 64.8 us  [the longest x1 31.6 us: body(): pl.pallas_call(functools.partial(second_kernel, shards, nb), out_shape=(s...]
    psum x4 -> x0, blocking collectives: 62.6 us -> none  [body(): encoded, energy_sum = lax.psum((partial_code, partial_energy), 'vel')]
    mul x3 -> x0, other arithmetic: 30 us -> none  [the longest x2 29.3 us: advect(): flux = courant * jnp.where(courant >= 0.0, forward, backward)]
    ppermute x4 -> x14, waiting for transfers between devices: 4.67 us -> 23.9 us  [shifted(): lax.ppermute(array, axes, [(i, (i + shift) % count) for i in range(count)])]
    ppermute x4 -> x14, starting transfers between devices: 4.32 us -> 19 us  [shifted(): lax.ppermute(array, axes, [(i, (i + shift) % count) for i in range(count)])]
    sub x2 -> x0, other arithmetic: 9.98 us -> none  [advect(): return padded[2:length + 2] - (flux[1:] - flux[:-1])]
    convert_element_type x1 -> x0, other arithmetic: 7.47 us -> none  [body(): state = density.astype(jnp.float32)]
  transfers between devices with their start and end apart: 4 -> 14, of which waited for: 2 -> 13; matrix products, arithmetic and copies ran while one was open for 5% -> 0% of each run, Pallas kernels for 0% -> 0%
where the time goes in v2:
time: 115 us
  Pallas kernels  64.8 us (56%)
  waiting for transfers between devices  23.9 us (21%)
  starting transfers between devices  19 us (17%)
  local copies, waits for them, and re-layouts  3.87 us (3%)
  other arithmetic  2.89 us (3%)
    pallas_call x1, Pallas kernels, body(): pl.pallas_call(functools.partial(second_kernel, shards, nb), out_shape=(s...  31.6 us
    ppermute x14, waiting for transfers between devices, shifted(): lax.ppermute(array, axes, [(i, (i + shift) % count) for i in range(count)])  23.9 us
    ppermute x14, starting transfers between devices, shifted(): lax.ppermute(array, axes, [(i, (i + shift) % count) for i in range(count)])  19 us
    pallas_call x1, Pallas kernels, body(): pl.pallas_call(functools.partial(first_kernel, shards, nb), out_shape=(me...  16.6 us
    pallas_call x1, Pallas kernels, body(): pl.pallas_call(functools.partial(third_kernel, shards, nb), out_shape=sha...  16.6 us
  transfers between devices with their start and end apart: 14, of which 13 were waited for; matrix products, arithmetic and copies ran while one was open for 0% of the time, Pallas kernels for 0%

profile of v2, /device:TPU:0, one launch (start us, length us, event | category | flops | bytes accessed | tf_op | source)
XLA Modules:
  0.0 115.1 jit_solution(1313892270631125961)
XLA Ops:
  0.0 0.8 fusion.20
  1.1 1.3 %fusion.24 = (bf16[4,27648]{1,0:T(4,128)(2,1)S(1)}, bf16[4,27648]{1,0:T(4,128)(2,1)S(1)}) fusion(bf16[96,27648]{1,0:T(8,128)(2,1)} %density.3), kind=kLoop, calls=%fused_computation.39 | loop fusion | bytes 884736 | tf_op jit(solution)/shard_map/slice | solution.py:537
  2.6 0.5 collective-permute-start
  3.7 2.0 %collective-permute-start.1 = (bf16[4,27776]{1,0:T(4,128)(2,1)S(1)}, bf16[4,27776]{1,0:T(4,128)(2,1)S(1)}, u32[]{:S(2)}, u32[]{:S(2)}) collective-permute-start(bf16[4,27776]{1,0:T(4,128)(2,1)S(1)} %pad_maximum_fusion.1), channel_id=1, source_target_pairs={{0,3},{1,0},{2,1},{3,2},{4,7},{5,4},{6,5},{7,6},{8,11},{9,8},{10,9... | collective-permute-start | bytes 666632 | tf_op jit(solution)/shard_map/ppermute | solution.py:495
  5.7 3.1 %collective-permute-done.left = bf16[4,27776]{1,0:T(4,128)(2,1)S(1)} collective-permute-done((bf16[4,27776]{1,0:T(4,128)(2,1)S(1)}, bf16[4,27776]{1,0:T(4,128)(2,1)S(1)}, u32[]{:S(2)}, u32[]{:S(2)}) %collective-permute-start) | collective-permute-done | bytes 222240 | tf_op jit(solution)/shard_map/ppermute | solution.py:495
  8.7 2.2 %collective-permute-done.1.right = bf16[4,27776]{1,0:T(4,128)(2,1)S(1)} collective-permute-done((bf16[4,27776]{1,0:T(4,128)(2,1)S(1)}, bf16[4,27776]{1,0:T(4,128)(2,1)S(1)}, u32[]{:S(2)}, u32[]{:S(2)}) %collective-permute-start.1) | collective-permute-done | bytes 222240 | tf_op jit(solution)/shard_map/ppermute | solution.py:495
  10.9 0.7 copy-done.3
  11.6 16.6 %first.1 = (f32[32,512]{1,0:T(8,128)}, f32[32,512]{1,0:T(8,128)}, f32[32,512]{1,0:T(8,128)}, f32[32,512]{1,0:T(8,128)}) custom-call(s32[24]{0:T(128)} %blocks.5, s32[4]{0:T(128)} %flags.3, bf16[96,27648]{1,0:T(8,128)(2,1)} %density.3, bf16[4,27776]{1,0:T(4,128)(2,1)} %copy-done.2, bf16[4,27776]{1,0:T(4,128)(2,1)} %copy-done.3, f32[1,27648]{1,0:T(1,128)} %bitcast.16, ...), custom_call_target="tpu_custom_call" | custom-call | tf_op jit(solution)/shard_map/first/pallas_call | solution.py:549
  28.2 1.6 %collective-permute-start.2 = (f32[32,512]{1,0:T(8,128)}, f32[32,512]{1,0:T(8,128)S(1)}, u32[]{:S(2)}, u32[]{:S(2)}) collective-permute-start(f32[32,512]{1,0:T(8,128)} %get-tuple-element.15), channel_id=1, source_target_pairs={{0,4},{4,8},{8,12},{12,0},{1,5},{5,9},{9,13},{13,1},{2,6},{6,10},{... | collective-permute-start | bytes 196616 | tf_op jit(solution)/shard_map/ppermute | solution.py:495
  29.9 2.6 %collective-permute-start.3 = (f32[32,512]{1,0:T(8,128)}, f32[32,512]{1,0:T(8,128)S(1)}, u32[]{:S(2)}, u32[]{:S(2)}) collective-permute-start(f32[32,512]{1,0:T(8,128)} %get-tuple-element.16), channel_id=1, source_target_pairs={{0,8},{4,12},{8,0},{12,4},{1,9},{5,13},{9,1},{13,5},{2,10},{6,14},... | collective-permute-start | bytes 196616 | tf_op jit(solution)/shard_map/ppermute | solution.py:495
  32.5 1.3 %collective-permute-start.4 = (f32[32,512]{1,0:T(8,128)}, f32[32,512]{1,0:T(8,128)S(1)}, u32[]{:S(2)}, u32[]{:S(2)}) collective-permute-start(f32[32,512]{1,0:T(8,128)} %get-tuple-element.17), channel_id=1, source_target_pairs={{0,12},{4,0},{8,4},{12,8},{1,13},{5,1},{9,5},{13,9},{2,14},{6,2},{... | collective-permute-start | bytes 196616 | tf_op jit(solution)/shard_map/ppermute | solution.py:495
  33.8 1.5 %collective-permute-done.2 = f32[32,512]{1,0:T(8,128)S(1)} collective-permute-done((f32[32,512]{1,0:T(8,128)}, f32[32,512]{1,0:T(8,128)S(1)}, u32[]{:S(2)}, u32[]{:S(2)}) %collective-permute-start.2) | collective-permute-done | bytes 65568 | tf_op jit(solution)/shard_map/ppermute | solution.py:495
  35.3 2.8 %collective-permute-done.3 = f32[32,512]{1,0:T(8,128)S(1)} collective-permute-done((f32[32,512]{1,0:T(8,128)}, f32[32,512]{1,0:T(8,128)S(1)}, u32[]{:S(2)}, u32[]{:S(2)}) %collective-permute-start.3) | collective-permute-done | bytes 65568 | tf_op jit(solution)/shard_map/ppermute | solution.py:495
  38.3 0.9 add_add_fusion.1.mine
  39.4 2.8 %collective-permute-start.7 = (bf16[32,512]{1,0:T(8,128)(2,1)S(1)}, bf16[32,512]{1,0:T(8,128)(2,1)S(1)}, u32[]{:S(2)}, u32[]{:S(2)}) collective-permute-start(bf16[32,512]{1,0:T(8,128)(2,1)S(1)} %fusion.2.refs_0_), channel_id=1, source_target_pairs={{0,12},{4,0},{8,4},{12,8},{1,13},{5,1},{9,5},{13,9},{2,14},{6,2},{... | collective-permute-start | bytes 98312 | tf_op jit(solution)/shard_map/ppermute | solution.py:495
  42.2 0.4 collective-permute-start.6
  42.8 1.0 collective-permute-done.7.refs_3_
  43.8 3.4 %collective-permute-done.6.refs_2_ = bf16[32,512]{1,0:T(8,128)(2,1)S(1)} collective-permute-done((bf16[32,512]{1,0:T(8,128)(2,1)S(1)}, bf16[32,512]{1,0:T(8,128)(2,1)S(1)}, u32[]{:S(2)}, u32[]{:S(2)}) %collective-permute-start.6) | collective-permute-done | bytes 32800 | tf_op jit(solution)/shard_map/ppermute | solution.py:495
  47.2 1.1 collective-permute-done.5.refs_1_
  48.3 0.6 copy-done.9
  48.9 31.6 %second.1 = (bf16[96,27648]{1,0:T(8,128)(2,1)}, f32[32,512]{1,0:T(8,128)}, f32[32,512]{1,0:T(8,128)}, f32[32,512]{1,0:T(8,128)}, f32[32,512]{1,0:T(8,128)}) custom-call(s32[24]{0:T(128)} %blocks.5, s32[4]{0:T(128)} %flags.3, bf16[96,27648]{1,0:T(8,128)(2,1)} %density.3, bf16[4,27776]{1,0:T(4,128)(2,1)} %copy-done.2, bf16[4,27776]{1,0:T(4,128)(2,1)} %copy-done.3, ...), custom_call_target="tpu_custom_call" | custom-call | tf_op jit(solution)/shard_map/second/pallas_call | solution.py:572
  80.6 0.9 collective-permute-start.9
  81.5 3.0 %collective-permute-start.10 = (f32[32,512]{1,0:T(8,128)}, f32[32,512]{1,0:T(8,128)S(1)}, u32[]{:S(2)}, u32[]{:S(2)}) collective-permute-start(f32[32,512]{1,0:T(8,128)} %get-tuple-element.22), channel_id=1, source_target_pairs={{0,12},{4,0},{8,4},{12,8},{1,13},{5,1},{9,5},{13,9},{2,14},{6,2},{... | collective-permute-start | bytes 196616 | tf_op jit(solution)/shard_map/ppermute | solution.py:495
  84.4 2.6 %collective-permute-done.8 = f32[32,512]{1,0:T(8,128)S(1)} collective-permute-done((f32[32,512]{1,0:T(8,128)}, f32[32,512]{1,0:T(8,128)S(1)}, u32[]{:S(2)}, u32[]{:S(2)}) %collective-permute-start.8) | collective-permute-done | bytes 65568 | tf_op jit(solution)/shard_map/ppermute | solution.py:495
  87.0 0.9 collective-permute-done.9
  87.9 0.9 add_add_fusion.energies
  89.0 2.9 %collective-permute-start.13 = (bf16[32,512]{1,0:T(8,128)(2,1)S(1)}, bf16[32,512]{1,0:T(8,128)(2,1)S(1)}, u32[]{:S(2)}, u32[]{:S(2)}) collective-permute-start(bf16[32,512]{1,0:T(8,128)(2,1)S(1)} %fusion.3.refs_0_), channel_id=1, source_target_pairs={{0,12},{4,0},{8,4},{12,8},{1,13},{5,1},{9,5},{13,9},{2,14},{6,2},{... | collective-permute-start | bytes 98312 | tf_op jit(solution)/shard_map/ppermute | solution.py:495
  92.5 1.0 collective-permute-done.13.refs_3_
  93.5 3.2 %collective-permute-done.12.refs_2_ = bf16[32,512]{1,0:T(8,128)(2,1)S(1)} collective-permute-done((bf16[32,512]{1,0:T(8,128)(2,1)S(1)}, bf16[32,512]{1,0:T(8,128)(2,1)S(1)}, u32[]{:S(2)}, u32[]{:S(2)}) %collective-permute-start.12) | collective-permute-done | bytes 32800 | tf_op jit(solution)/shard_map/ppermute | solution.py:495
  96.7 1.1 collective-permute-done.11.refs_1_
  97.8 0.6 copy-done.12
  98.4 16.6 %third.1 = bf16[96,27648]{1,0:T(8,128)(2,1)} custom-call(s32[24]{0:T(128)} %blocks.5, bf16[96,27648]{1,0:T(8,128)(2,1)} %get-tuple-element.18.source, bf16[27648,512]{1,0:T(8,128)(2,1)} %coder.5, f32[32,512]{1,0:T(8,128)} %copy-done.1, f32[32,512]{1,0:T(8,128)} %copy-done.4, f32[1,96]{1,0:T(1,128)} %bitcast.19, bf16[32,512]{1,0:T(8,128)(2,1)} %copy-done.6, ...), custom_call_target="tpu_custom_call" | custom-call | tf_op jit(solution)/shard_map/third/pallas_call | solution.py:602
  (43 shorter events, 2.6 us)
Async XLA Ops:
  0.0 39.1 %copy-start = (bf16[512,512]{1,0:T(8,128)(2,1)S(1)}, bf16[512,512]{1,0:T(8,128)(2,1)}, u32[]{:S(2)}) copy-start(bf16[512,512]{1,0:T(8,128)(2,1)} %param.10) | copy-start | bytes 1572868
  2.6 6.1 %collective-permute-start = (bf16[4,27776]{1,0:T(4,128)(2,1)S(1)}, bf16[4,27776]{1,0:T(4,128)(2,1)S(1)}, u32[]{:S(2)}, u32[]{:S(2)}) collective-permute-start(bf16[4,27776]{1,0:T(4,128)(2,1)S(1)} %pad_maximum_fusion), channel_id=1, source_target_pairs={{0,1},{1,2},{2,3},{3,0},{4,5},{5,6},{6,7},{7,4},{8,9},{9,10},{10,1... | collective-permute-start | bytes 666632 | tf_op jit(solution)/shard_map/ppermute | solution.py:495
  3.7 7.2 %collective-permute-start.1 = (bf16[4,27776]{1,0:T(4,128)(2,1)S(1)}, bf16[4,27776]{1,0:T(4,128)(2,1)S(1)}, u32[]{:S(2)}, u32[]{:S(2)}) collective-permute-start(bf16[4,27776]{1,0:T(4,128)(2,1)S(1)} %pad_maximum_fusion.1), channel_id=1, source_target_pairs={{0,3},{1,0},{2,1},{3,2},{4,7},{5,4},{6,5},{7,6},{8,11},{9,8},{10,9... | collective-permute-start | bytes 666632 | tf_op jit(solution)/shard_map/ppermute | solution.py:495
  8.7 2.2 %copy-start.2 = (bf16[4,27776]{1,0:T(4,128)(2,1)}, bf16[4,27776]{1,0:T(4,128)(2,1)S(1)}, u32[]{:S(2)}) copy-start(bf16[4,27776]{1,0:T(4,128)(2,1)S(1)} %collective-permute-done.left) | copy-start | bytes 666628
  10.9 0.7 copy-start.3
  11.6 27.5 %copy-start.13 = (f32[512]{0:T(512)S(1)}, f32[512]{0:T(512)}, u32[]{:S(2)}) copy-start(f32[512]{0:T(512)} %param.11) | copy-start | bytes 6148
  28.2 7.1 %collective-permute-start.2 = (f32[32,512]{1,0:T(8,128)}, f32[32,512]{1,0:T(8,128)S(1)}, u32[]{:S(2)}, u32[]{:S(2)}) collective-permute-start(f32[32,512]{1,0:T(8,128)} %get-tuple-element.15), channel_id=1, source_target_pairs={{0,4},{4,8},{8,12},{12,0},{1,5},{5,9},{9,13},{13,1},{2,6},{6,10},{... | collective-permute-start | bytes 196616 | tf_op jit(solution)/shard_map/ppermute | solution.py:495
  29.9 8.2 %collective-permute-start.3 = (f32[32,512]{1,0:T(8,128)}, f32[32,512]{1,0:T(8,128)S(1)}, u32[]{:S(2)}, u32[]{:S(2)}) collective-permute-start(f32[32,512]{1,0:T(8,128)} %get-tuple-element.16), channel_id=1, source_target_pairs={{0,8},{4,12},{8,0},{12,4},{1,9},{5,13},{9,1},{13,5},{2,10},{6,14},... | collective-permute-start | bytes 196616 | tf_op jit(solution)/shard_map/ppermute | solution.py:495
  32.5 5.8 %collective-permute-start.4 = (f32[32,512]{1,0:T(8,128)}, f32[32,512]{1,0:T(8,128)S(1)}, u32[]{:S(2)}, u32[]{:S(2)}) collective-permute-start(f32[32,512]{1,0:T(8,128)} %get-tuple-element.17), channel_id=1, source_target_pairs={{0,12},{4,0},{8,4},{12,8},{1,13},{5,1},{9,5},{13,9},{2,14},{6,2},{... | collective-permute-start | bytes 196616 | tf_op jit(solution)/shard_map/ppermute | solution.py:495
  39.1 9.2 %copy-start.1 = (f32[32,512]{1,0:T(8,128)}, f32[32,512]{1,0:T(8,128)S(1)}, u32[]{:S(2)}) copy-start(f32[32,512]{1,0:T(8,128)S(1)} %add_add_fusion.1.mine) | copy-start | bytes 196612
  39.4 9.0 %copy-start.5 = (bf16[32,512]{1,0:T(8,128)(2,1)}, bf16[32,512]{1,0:T(8,128)(2,1)S(1)}, u32[]{:S(2)}) copy-start(bf16[32,512]{1,0:T(8,128)(2,1)S(1)} %fusion.2.refs_0_) | copy-start | bytes 98308
  39.4 4.4 %collective-permute-start.7 = (bf16[32,512]{1,0:T(8,128)(2,1)S(1)}, bf16[32,512]{1,0:T(8,128)(2,1)S(1)}, u32[]{:S(2)}, u32[]{:S(2)}) collective-permute-start(bf16[32,512]{1,0:T(8,128)(2,1)S(1)} %fusion.2.refs_0_), channel_id=1, source_target_pairs={{0,12},{4,0},{8,4},{12,8},{1,13},{5,1},{9,5},{13,9},{2,14},{6,2},{... | collective-permute-start | bytes 98312 | tf_op jit(solution)/shard_map/ppermute | solution.py:495
  42.2 5.0 %collective-permute-start.6 = (bf16[32,512]{1,0:T(8,128)(2,1)S(1)}, bf16[32,512]{1,0:T(8,128)(2,1)S(1)}, u32[]{:S(2)}, u32[]{:S(2)}) collective-permute-start(bf16[32,512]{1,0:T(8,128)(2,1)S(1)} %fusion.2.refs_0_), channel_id=1, source_target_pairs={{0,8},{4,12},{8,0},{12,4},{1,9},{5,13},{9,1},{13,5},{2,10},{6,14},... | collective-permute-start | bytes 98312 | tf_op jit(solution)/shard_map/ppermute | solution.py:495
  42.6 5.7 %collective-permute-start.5 = (bf16[32,512]{1,0:T(8,128)(2,1)S(1)}, bf16[32,512]{1,0:T(8,128)(2,1)S(1)}, u32[]{:S(2)}, u32[]{:S(2)}) collective-permute-start(bf16[32,512]{1,0:T(8,128)(2,1)S(1)} %fusion.2.refs_0_), channel_id=1, source_target_pairs={{0,4},{4,8},{8,12},{12,0},{1,5},{5,9},{9,13},{13,1},{2,6},{6,10},{... | collective-permute-start | bytes 98312 | tf_op jit(solution)/shard_map/ppermute | solution.py:495
  43.8 4.5 %copy-start.7 = (bf16[32,512]{1,0:T(8,128)(2,1)}, bf16[32,512]{1,0:T(8,128)(2,1)S(1)}, u32[]{:S(2)}) copy-start(bf16[32,512]{1,0:T(8,128)(2,1)S(1)} %collective-permute-done.7.refs_3_) | copy-start | bytes 98308
  47.2 1.1 copy-start.8
  48.3 0.6 copy-start.9
  80.5 6.5 %collective-permute-start.8 = (f32[32,512]{1,0:T(8,128)}, f32[32,512]{1,0:T(8,128)S(1)}, u32[]{:S(2)}, u32[]{:S(2)}) collective-permute-start(f32[32,512]{1,0:T(8,128)} %get-tuple-element.20), channel_id=1, source_target_pairs={{0,4},{4,8},{8,12},{12,0},{1,5},{5,9},{9,13},{13,1},{2,6},{6,10},{... | collective-permute-start | bytes 196616 | tf_op jit(solution)/shard_map/ppermute | solution.py:495
  80.6 7.3 %collective-permute-start.9 = (f32[32,512]{1,0:T(8,128)}, f32[32,512]{1,0:T(8,128)S(1)}, u32[]{:S(2)}, u32[]{:S(2)}) collective-permute-start(f32[32,512]{1,0:T(8,128)} %get-tuple-element.21), channel_id=1, source_target_pairs={{0,8},{4,12},{8,0},{12,4},{1,9},{5,13},{9,1},{13,5},{2,10},{6,14},... | collective-permute-start | bytes 196616 | tf_op jit(solution)/shard_map/ppermute | solution.py:495
  81.5 6.4 %collective-permute-start.10 = (f32[32,512]{1,0:T(8,128)}, f32[32,512]{1,0:T(8,128)S(1)}, u32[]{:S(2)}, u32[]{:S(2)}) collective-permute-start(f32[32,512]{1,0:T(8,128)} %get-tuple-element.22), channel_id=1, source_target_pairs={{0,12},{4,0},{8,4},{12,8},{1,13},{5,1},{9,5},{13,9},{2,14},{6,2},{... | collective-permute-start | bytes 196616 | tf_op jit(solution)/shard_map/ppermute | solution.py:495
  88.7 9.1 %copy-start.4 = (f32[32,512]{1,0:T(8,128)}, f32[32,512]{1,0:T(8,128)S(1)}, u32[]{:S(2)}) copy-start(f32[32,512]{1,0:T(8,128)S(1)} %add_add_fusion.energies) | copy-start | bytes 196612
  89.0 8.8 %copy-start.6 = (bf16[32,512]{1,0:T(8,128)(2,1)}, bf16[32,512]{1,0:T(8,128)(2,1)S(1)}, u32[]{:S(2)}) copy-start(bf16[32,512]{1,0:T(8,128)(2,1)S(1)} %fusion.3.refs_0_) | copy-start | bytes 98308
  89.0 4.5 %collective-permute-start.13 = (bf16[32,512]{1,0:T(8,128)(2,1)S(1)}, bf16[32,512]{1,0:T(8,128)(2,1)S(1)}, u32[]{:S(2)}, u32[]{:S(2)}) collective-permute-start(bf16[32,512]{1,0:T(8,128)(2,1)S(1)} %fusion.3.refs_0_), channel_id=1, source_target_pairs={{0,12},{4,0},{8,4},{12,8},{1,13},{5,1},{9,5},{13,9},{2,14},{6,2},{... | collective-permute-start | bytes 98312 | tf_op jit(solution)/shard_map/ppermute | solution.py:495
  91.8 4.8 %collective-permute-start.12 = (bf16[32,512]{1,0:T(8,128)(2,1)S(1)}, bf16[32,512]{1,0:T(8,128)(2,1)S(1)}, u32[]{:S(2)}, u32[]{:S(2)}) collective-permute-start(bf16[32,512]{1,0:T(8,128)(2,1)S(1)} %fusion.3.refs_0_), channel_id=1, source_target_pairs={{0,8},{4,12},{8,0},{12,4},{1,9},{5,13},{9,1},{13,5},{2,10},{6,14},... | collective-permute-start | bytes 98312 | tf_op jit(solution)/shard_map/ppermute | solution.py:495
  92.1 5.7 %collective-permute-start.11 = (bf16[32,512]{1,0:T(8,128)(2,1)S(1)}, bf16[32,512]{1,0:T(8,128)(2,1)S(1)}, u32[]{:S(2)}, u32[]{:S(2)}) collective-permute-start(bf16[32,512]{1,0:T(8,128)(2,1)S(1)} %fusion.3.refs_0_), channel_id=1, source_target_pairs={{0,4},{4,8},{8,12},{12,0},{1,5},{5,9},{9,13},{13,1},{2,6},{6,10},{... | collective-permute-start | bytes 98312 | tf_op jit(solution)/shard_map/ppermute | solution.py:495
  93.4 4.3 %copy-start.10 = (bf16[32,512]{1,0:T(8,128)(2,1)}, bf16[32,512]{1,0:T(8,128)(2,1)S(1)}, u32[]{:S(2)}) copy-start(bf16[32,512]{1,0:T(8,128)(2,1)S(1)} %collective-permute-done.13.refs_3_) | copy-start | bytes 98308
  96.7 1.1 copy-start.11
  97.8 0.6 copy-start.12

commit v3 on v2

v3 whole, which is shorter than its diff:
```python
import functools
import math

import jax
import jax.numpy as jnp
import numpy as np
from jax import lax
from jax.experimental import pallas as pl
from jax.experimental.pallas import tpu as pltpu
from jax.sharding import PartitionSpec as P

VGRID = 48
LATENT = 512
VBLOCKS = 96
STEPS = 2
VELS = 110592
WIDTH = VELS // VBLOCKS
LANES = 128
HALO = 4
RING = 4
GROUP = 9
VMEM_MIB = 57
SINK_RATE = 0.5
COURANT = 0.9
SCALE = math.sqrt(VELS / LATENT)
F32 = jnp.float32
BF16 = jnp.bfloat16


def grid_moments():
    centres = (2.0 * np.arange(VGRID) + 1.0 - VGRID) / VGRID
    second = float(np.sum(centres**2))
    fourth = float(np.sum(centres**4))
    number = float(VGRID)
    total = number**3
    cross = 3.0 * number * number * second
    quartic = 3.0 * number * number * fourth + 6.0 * number * second * second
    square = number * number * second
    return (total, cross, quartic, square)


def moment_pattern(pats):
    number = lax.broadcasted_iota(jnp.int32, (1, WIDTH), 1).astype(F32)
    along_y = jnp.floor((number + 0.5) * (1.0 / VGRID))
    along_z = number - VGRID * along_y
    first = 2.0 * along_y + (1 - VGRID)
    pats[0:1, :] = first
    pats[1:2, :] = first + (2 * WIDTH // VGRID)
    pats[2:3, :] = 2.0 * along_z + (1 - VGRID)


def taps(block):
    along = 2 * (block * WIDTH // (VGRID * VGRID)) + 1 - VGRID
    sign = jnp.where(along >= 0, 1, -1)
    along = along.astype(F32)
    a = jnp.abs(along) * (COURANT / VGRID)
    upwind = (1.0 - a) * 0.5
    curved = (1.0 - a * a) * (1.0 / 6.0)
    far = -a * curved
    behind = a * (1.0 - upwind + 3.0 * curved)
    here = 1.0 - a * (1.0 - 2.0 * upwind + 3.0 * curved)
    ahead = -a * (upwind - curved)
    return along, sign, (far, behind, here, ahead)


def stencil(ref, tile, first, count, sign, weights):
    far, behind, here, ahead = weights
    at = lambda shift: ref[tile, pl.ds(first + shift, count), :]
    return (
        far * at(-2 * sign) + behind * at(-sign) + here * at(0) + ahead * at(sign)
    )


def fill(pad, tile, lanes, far_lanes, density, left, right, inflow, open_left, open_right):
    cells = density.shape[0]
    ghost = inflow[:, far_lanes]
    pad[tile, 8 : 8 + cells, :] = density[:, lanes].astype(F32)
    pad[tile, 8 - HALO : 8, :] = jnp.where(open_left, left[:, far_lanes].astype(F32), ghost)
    pad[tile, 8 + cells : 8 + cells + HALO, :] = jnp.where(
        open_right, right[:, far_lanes].astype(F32), ghost
    )


def energy_row(total, rows):
    column = jnp.sum(total, axis=1, keepdims=True) * (1.0 / (VGRID * VGRID))
    row = lax.broadcasted_iota(jnp.int32, (rows, LANES), 0)
    lane = lax.broadcasted_iota(jnp.int32, (rows, LANES), 1)
    return jnp.sum(jnp.where(row == lane, column, 0.0), axis=0, keepdims=True)


def pattern_rows(pats, parity, lanes):
    y = jnp.where(parity == 0, pats[0:1, lanes], pats[1:2, lanes])
    return y, pats[2:3, lanes]


def sides(flags):
    sub_count = lax.axis_size("sub")
    count = lax.axis_size("cell") * sub_count
    position = lax.axis_index("cell") * sub_count + lax.axis_index("sub")
    return flags[position] == 1, flags[lax.rem(position + 1, count)] == 1


class Stream:
    def __init__(self, source, buffers, sems, tile, axis, inward=True):
        self.source, self.buffers, self.sems = source, buffers, sems
        self.tile, self.axis, self.inward = tile, axis, inward
        self.count = source.shape[axis] // tile
        self.slots = buffers.shape[0]

    def copy(self, i, u):
        slot = u % self.slots
        span = pl.ds(pl.multiple_of(i * self.tile, LANES), self.tile)
        far = self.source.at[span, :] if self.axis == 0 else self.source.at[:, span]
        near = self.buffers.at[slot]
        source, target = (far, near) if self.inward else (near, far)
        return pltpu.make_async_copy(source, target, self.sems.at[slot])

    def begin(self, ahead):
        for i in range(min(ahead, self.count)):
            self.copy(i, i).start()

    def start(self, i, u):
        if isinstance(i, int):
            if i < self.count:
                self.copy(i, u).start()
        else:

            @pl.when(i < self.count)
            def _():
                self.copy(i, u).start()

    def wait(self, i, u):
        self.copy(i, u).wait()

    def drain(self, i, u):
        if isinstance(i, int):
            if i >= self.slots:
                self.wait(i - self.slots, u)
        else:

            @pl.when(i >= self.slots)
            def _():
                self.wait(i - self.slots, u)

    def at(self, u):
        return self.buffers.at[u % self.slots]


def unrolled(first, last, step):
    trips = (last - first) // RING
    if trips > 1:

        def trip(j, carry):
            for k in range(RING):
                step(first + RING * j + k, (first + k) % RING)
            return carry

        lax.fori_loop(0, trips, trip, 0)
        first = first + RING * trips
    for i in range(first, last):
        step(i, i % RING)


def put_parts(message, row_of, values, count, lane_step=0):
    height, width = values.shape
    for k in range(count):
        part = values.astype(BF16)
        values = values - part.astype(F32)
        for r in range(height):
            lanes = slice(k * lane_step, k * lane_step + width)
            message[row_of(k, r) : row_of(k, r) + 1, lanes] = part[r : r + 1]


def moment_row(rows, k, r):
    place = 5 * k + r
    return rows + place if place < 8 else rows - 2 + (place - 8)


def first_kernel(nb, blocks, flags, density, left, right, inflow, coder, message, *refs):
    pad, coarse_a, coarse_b, energy, pats, sums, tiles_c, sem_c, tiles_d, sem_d = refs
    cells = density.shape[0]
    rows = cells + 2 * HALO
    width = nb * WIDTH
    tiles = WIDTH // LANES
    coders = Stream(coder, tiles_c, sem_c, width, 0)
    cells_in = Stream(density, tiles_d, sem_d, width, 1)
    cells_in.begin(1)
    coders.begin(RING - 1)
    for i in range(1, min(RING - 1, cells_in.count)):
        cells_in.copy(i, i).start()
    steps = coders.count
    coarse = (coarse_a, coarse_b)

    moment_pattern(pats)
    sums[...] = jnp.zeros_like(sums)
    energy[...] = jnp.zeros_like(energy)
    pad[...] = jnp.zeros_like(pad)
    open_left, open_right = sides(flags)
    kind = lax.broadcasted_iota(jnp.int32, (8, LANES), 0)

    def transport(i, u):
        source = cells_in.at(u)
        for k in range(nb):
            block = blocks[i * nb + k]
            along, sign, weights = taps(block)
            parity = lax.rem(block, 2)
            total = energy[...]
            for t in range(tiles):
                tile = k * tiles + t
                lanes = slice(tile * LANES, (tile + 1) * LANES)
                far = pl.ds(pl.multiple_of(i * width + tile * LANES, LANES), LANES)
                fill(pad, tile, lanes, far, source, left, right, inflow, open_left, open_right)
                fstar = stencil(pad, tile, 8 - HALO, rows, sign, weights)
                y, z = pattern_rows(pats, parity, slice(t * LANES, (t + 1) * LANES))
                e = along * along + (y * y + z * z)
                total = total + fstar * e
                high = e.astype(BF16).astype(F32)
                basis = jnp.where(kind == 0, 1.0, 0.0)
                basis = jnp.where(kind == 1, along, basis)
                basis = jnp.where(kind == 2, y, basis)
                basis = jnp.where(kind == 3, z, basis)
                basis = jnp.where(kind == 4, high, basis)
                basis = jnp.where(kind == 5, e - high, basis)
                coarse[u % 2][:, lanes] = jnp.concatenate([fstar, basis], 0).astype(BF16)
            energy[...] = total

    def encode(u):
        sums[...] += jnp.dot(coarse[u % 2][...], coders.at(u)[...], preferred_element_type=F32)

    def step(i, u):
        cells_in.wait(i, u)
        coders.wait(i, u)
        coders.start(i + RING - 2, u + RING - 2)
        cells_in.start(i + RING - 2, u + RING - 2)
        encode(u + RING - 1)
        transport(i, u)

    cells_in.wait(0, 0)
    transport(0, 0)
    coders.wait(0, 0)
    unrolled(1, steps, step)
    encode(steps - 1)

    message[0:rows, :] = sums[0:rows, :].astype(BF16)
    last = sums[rows + 4 : rows + 5, :] + sums[rows + 5 : rows + 6, :]
    moments = jnp.concatenate([sums[rows : rows + 4, :], last], 0)
    put_parts(message, functools.partial(moment_row, rows), moments, 2)
    put_parts(message, lambda k, r: 0, energy_row(energy[...], rows), 3, LANES)


def project(act, moments, energy, restitution, pats, consts, bands):
    total, cross, quartic, square = grid_moments()
    determinant = total * quartic - cross * cross
    rows = restitution.shape[0]
    inverse = 1.0 / VGRID
    dots = [
        SCALE * jnp.sum(act * moments[k : k + 1, :], axis=1, keepdims=True) for k in range(5)
    ]
    row = lax.broadcasted_iota(jnp.int32, (rows, LANES), 0)
    lane = lax.broadcasted_iota(jnp.int32, (rows, LANES), 1)
    energy_sum = jnp.sum(jnp.where(row == lane, energy, 0.0), axis=1, keepdims=True)
    sink = -SINK_RATE * (1.0 - restitution * restitution) * energy_sum
    excess = dots[4] * (inverse * inverse) - sink
    mass = (quartic * dots[0] - cross * excess) / determinant
    power = (total * excess - cross * dots[0]) / determinant * (inverse * inverse)
    slopes = [dots[k] * (inverse * inverse / square) for k in (1, 2, 3)]
    spread = lambda column: jnp.broadcast_to(column, (rows, LANES))
    consts[0] = spread(mass)
    consts[1] = spread(slopes[0])
    consts[2] = spread(power)
    power, second, third = spread(power), spread(slopes[1]), spread(slopes[2])
    for parity in range(2):
        for t in range(WIDTH // LANES):
            lanes = slice(t * LANES, (t + 1) * LANES)
            y, z = pats[parity : parity + 1, lanes], pats[2:3, lanes]
            bands[parity, t] = second * y + third * z + power * (y * y + z * z)


def diagonal(row, first, rows):
    shape = (rows, row.shape[1])
    place = lax.broadcasted_iota(jnp.int32, shape, 0) - first
    lane = lax.broadcasted_iota(jnp.int32, shape, 1)
    return jnp.sum(jnp.where(place == lane, row, 0.0), axis=1, keepdims=True)


def collect(message, others, total):
    total[...] = message[...].astype(F32)
    for other in others:
        total[...] += other[...].astype(F32)


def energy_of(total, row):
    return sum(total[row : row + 1, k * LANES : (k + 1) * LANES] for k in range(3))


def latent_layer(total, w_latent, b_latent, active):
    mixed = jnp.dot(total[...].astype(BF16), w_latent[...], preferred_element_type=F32)
    active[...] = jnp.tanh(mixed + b_latent[...]).astype(BF16)


def diagonal(row, first, rows):
    shape = (rows, row.shape[1])
    place = lax.broadcasted_iota(jnp.int32, shape, 0) - first
    lane = lax.broadcasted_iota(jnp.int32, shape, 1)
    return jnp.sum(jnp.where(place == lane, row, 0.0), axis=1, keepdims=True)


def second_kernel(
    nb, peers, blocks, flags, density, left, right, inflow, coder, w_latent, b_latent,
    restitution, *refs
):
    parts, refs = refs[:peers], refs[peers:]
    (
        out, message, moments, pad, state, decoded_a, decoded_b, coarse, energy, pats, sums,
        total, active, consts, bands, weights_in, sem_w,
        tiles_c, sem_c, tiles_d, sem_d, sem_o,
    ) = refs
    cells = density.shape[0]
    rows = cells + 2 * HALO
    width = nb * WIDTH
    tiles = WIDTH // LANES
    load = pltpu.make_async_copy(w_latent, weights_in, sem_w)
    load.start()
    coders = Stream(coder, tiles_c, sem_c, width, 0)
    cells_in = Stream(density, tiles_d, sem_d, width, 1)
    cells_out = Stream(out, coarse, sem_o, width, 1, inward=False)
    coders.begin(RING - 1)
    cells_in.begin(RING - 1)
    steps = coders.count
    decoded = (decoded_a, decoded_b)
    vels = density.shape[1]

    collect(parts[0], parts[1:], total)
    moment_pattern(pats)
    sums[...] = jnp.zeros_like(sums)
    energy[...] = jnp.zeros_like(energy)
    pad[...] = jnp.zeros_like(pad)
    open_left, open_right = sides(flags)
    for r in range(5):
        at = [moment_row(rows, k, r) for k in range(2)]
        moments[r : r + 1, :] = total[at[0] : at[0] + 1, :] + total[at[1] : at[1] + 1, :]
    ghosts = [jnp.sum(side[:, vels:].astype(F32), axis=1, keepdims=True) for side in (left, right)]
    r = diagonal(restitution[...], HALO, rows)
    state[0, 0:rows, :] = jnp.broadcast_to(r, (rows, LANES))
    state[0, 0:HALO, :] = jnp.broadcast_to(ghosts[0], (HALO, LANES))
    state[0, HALO + cells : rows, :] = jnp.broadcast_to(ghosts[1], (HALO, LANES))
    load.wait()
    latent_layer(total, weights_in, b_latent, active)
    project(
        active[0:rows, :].astype(F32), moments, energy_of(total, 0), state[0, :, 0:1],
        pats, consts, bands,
    )
    place = lax.broadcasted_iota(jnp.int32, (8, LANES), 0)
    cut_top = jnp.logical_and(place < HALO, jnp.logical_not(open_left))
    cut_bottom = jnp.logical_and(place >= 8 - HALO, jnp.logical_not(open_right))

    def decode_part(u, tile, count):
        span = slice(tile * LANES, (tile + count) * LANES)
        decoded[u % 2][:, span] = lax.dot_general(
            active[...], coders.at(u)[span, :], (((1,), (1,)), ((), ())),
            preferred_element_type=F32,
        )

    def encode_part(u, tile, count):
        span = slice(tile * LANES, (tile + count) * LANES)
        sums[...] += jnp.dot(
            cells_out.at(u)[:, span], coders.at(u)[span, :], preferred_element_type=F32
        )

    def transport(i, u, between):
        source = cells_in.at(u)
        target = cells_out.at(u)
        for k in range(nb):
            block = blocks[i * nb + k]
            along, sign, weights = taps(block)
            parity = lax.rem(block, 2)
            level = consts[0] + along * consts[1] + (along * along) * consts[2]
            total = energy[...]
            for t in range(tiles):
                tile = k * tiles + t
                between(tile)
                lanes = slice(tile * LANES, (tile + 1) * LANES)
                far = pl.ds(pl.multiple_of(i * width + tile * LANES, LANES), LANES)
                fill(pad, tile, lanes, far, source, left, right, inflow, open_left, open_right)
                fstar = stencil(pad, tile, 8 - HALO, rows, sign, weights)
                full = fstar + (
                    SCALE * decoded[u % 2][0:rows, lanes] - (level + bands[parity, t])
                )
                ghost = inflow[:, far]
                state[tile, 0:8, :] = jnp.where(cut_top, ghost, full[0:8])
                state[tile, 8 : rows - 8, :] = full[8 : rows - 8]
                state[tile, rows - 8 : rows, :] = jnp.where(cut_bottom, ghost, full[rows - 8 :])
                again = stencil(state, tile, HALO, cells, sign, weights)
                y, z = pattern_rows(pats, parity, slice(t * LANES, (t + 1) * LANES))
                total = total + again * (along * along + (y * y + z * z))
                target[:, lanes] = again.astype(BF16)
            energy[...] = total

    def step(i, u, before=True, after=True):
        cells_in.wait(i, u)
        if after:
            coders.wait(i + 1, u + 1)
        if before:
            coders.start(i + RING - 2, u + RING - 2)
        cells_in.start(i + RING - 1, u + RING - 1)
        cells_out.drain(i, u)

        def between(tile):
            if before and tile % GROUP == 0:
                encode_part(u + RING - 1, tile, GROUP)
            if after and tile % GROUP == 0:
                decode_part(u + 1, tile, GROUP)

        transport(i, u, between)
        cells_out.start(i, u)

    coders.wait(0, 0)
    decode_part(0, 0, nb * tiles)
    step(0, 0, before=False)
    unrolled(1, steps - 1, step)
    last = steps - 1
    step(last, last, after=False)
    encode_part(last, 0, nb * tiles)
    message[0:cells, :] = sums[...].astype(BF16)
    put_parts(message, lambda k, r: cells, energy_row(energy[...], cells), 3, LANES)
    for i in range(max(0, steps - cells_out.slots), steps):
        cells_out.wait(i, i)


def third_kernel(
    nb, peers, blocks, source, coder, w_latent, b_latent, moments, restitution, *refs
):
    parts, refs = refs[:peers], refs[peers:]
    (
        out, decoded_a, decoded_b, result, pats, total, active, consts, bands,
        weights_in, sem_w, tiles_c, sem_c, tiles_d, sem_d, sem_o,
    ) = refs
    cells = source.shape[0]
    width = nb * WIDTH
    tiles = WIDTH // LANES
    load = pltpu.make_async_copy(w_latent, weights_in, sem_w)
    load.start()
    coders = Stream(coder, tiles_c, sem_c, width, 0)
    cells_in = Stream(source, tiles_d, sem_d, width, 1)
    cells_out = Stream(out, result, sem_o, width, 1, inward=False)
    coders.begin(RING)
    cells_in.begin(RING - 1)
    steps = coders.count
    decoded = (decoded_a, decoded_b)

    collect(parts[0], parts[1:], total)
    moment_pattern(pats)
    load.wait()
    latent_layer(total, weights_in, b_latent, active)
    project(
        active[0:cells, :].astype(F32), moments, energy_of(total, cells),
        diagonal(restitution[...], 0, cells), pats, consts, bands,
    )

    def decode_part(u, tile, count):
        span = slice(tile * LANES, (tile + count) * LANES)
        decoded[u % 2][:, span] = lax.dot_general(
            active[0:cells, :], coders.at(u)[span, :], (((1,), (1,)), ((), ())),
            preferred_element_type=F32,
        )

    def finish(i, u, between):
        here = cells_in.at(u)
        target = cells_out.at(u)
        for k in range(nb):
            block = blocks[i * nb + k]
            along = (2 * (block * WIDTH // (VGRID * VGRID)) + 1 - VGRID).astype(F32)
            parity = lax.rem(block, 2)
            level = consts[0] + along * consts[1] + (along * along) * consts[2]
            for t in range(tiles):
                tile = k * tiles + t
                between(tile)
                lanes = slice(tile * LANES, (tile + 1) * LANES)
                full = here[:, lanes].astype(F32) + (
                    SCALE * decoded[u % 2][:, lanes] - (level + bands[parity, t])
                )
                target[:, lanes] = full.astype(BF16)

    def step(i, u, after=True):
        cells_in.wait(i, u)
        if after:
            coders.wait(i + 1, u + 1)
        coders.start(i + RING, u)
        cells_in.start(i + RING - 1, u + RING - 1)
        cells_out.drain(i, u)

        def between(tile):
            if after and tile % GROUP == 0:
                decode_part(u + 1, tile, GROUP)

        finish(i, u, between)
        cells_out.start(i, u)

    coders.wait(0, 0)
    decode_part(0, 0, nb * tiles)
    unrolled(0, steps - 1, step)
    step(steps - 1, steps - 1, after=False)
    for i in range(max(0, steps - cells_out.slots), steps):
        cells_out.wait(i, i)


def shifted(array, axes, count, shift):
    return lax.ppermute(array, axes, [(i, (i + shift) % count) for i in range(count)])


def pieces(values):
    first = lax.reduce_precision(values, 8, 7)
    second = lax.reduce_precision(values - first, 8, 7)
    third = values - first - second
    return jnp.stack([first, second, third], -1).astype(BF16)


def spread(message):
    count = lax.axis_size("vel")
    return [message] + [shifted(message, "vel", count, s) for s in range(1, count)]


def body(density, coder, w_latent, b_latent, restitution, inflow, flags, blocks):
    cells, vels = density.shape
    count = blocks.shape[0]
    nb = 2 if count % 2 == 0 else 1
    width = nb * WIDTH
    tiles = width // LANES
    rows = cells + 2 * HALO
    ring = ("cell", "sub")
    ring_count = lax.axis_size("cell") * lax.axis_size("sub")
    peers = lax.axis_size("vel")

    def edge(part, r):
        extra = jnp.pad(pieces(r), ((0, 0), (0, LANES - 3)))
        return jnp.concatenate([part, extra], 1)

    left = shifted(edge(density[cells - HALO :], restitution[cells - HALO :]), ring, ring_count, 1)
    right = shifted(edge(density[:HALO], restitution[:HALO]), ring, ring_count, -1)
    inflow = inflow[None, :]
    restitution = restitution[None, :]
    b_latent = b_latent[None, :]

    shape = jax.ShapeDtypeStruct
    vmem = pl.BlockSpec(memory_space=pltpu.VMEM)
    smem = pl.BlockSpec(memory_space=pltpu.SMEM)
    hbm = pl.BlockSpec(memory_space=pl.ANY)
    params = pltpu.CompilerParams(vmem_limit_bytes=VMEM_MIB * 1024 * 1024)
    dma = pltpu.SemaphoreType.DMA
    coder_ring = [pltpu.VMEM((RING, width, LATENT), BF16), dma((RING,))]
    cells_ring = [pltpu.VMEM((RING, cells, width), BF16), dma((RING,))]
    latent_in = [pltpu.VMEM((LATENT, LATENT), BF16), dma(())]

    message = pl.pallas_call(
        functools.partial(first_kernel, nb),
        out_shape=shape((rows + 8, LATENT), BF16),
        in_specs=[smem, smem, hbm, vmem, vmem, vmem, hbm],
        out_specs=vmem,
        scratch_shapes=[
            pltpu.VMEM((tiles, rows + 8, LANES), F32),
            pltpu.VMEM((rows + 8, width), BF16),
            pltpu.VMEM((rows + 8, width), BF16),
            pltpu.VMEM((rows, LANES), F32),
            pltpu.VMEM((8, WIDTH), F32),
            pltpu.VMEM((rows + 8, LATENT), F32),
            *coder_ring,
            *cells_ring,
        ],
        compiler_params=params,
        name="first",
    )(blocks, flags, density, left, right, inflow, coder)

    coarse, message, moments = pl.pallas_call(
        functools.partial(second_kernel, nb, peers),
        out_shape=(
            shape((cells, vels), BF16), shape((cells + 8, LATENT), BF16), shape((8, LATENT), F32),
        ),
        in_specs=[smem, smem, hbm, vmem, vmem, vmem, hbm, hbm, vmem, vmem] + [vmem] * peers,
        out_specs=(hbm, vmem, vmem),
        scratch_shapes=[
            pltpu.VMEM((tiles, rows + 8, LANES), F32),
            pltpu.VMEM((tiles, rows, LANES), F32),
            pltpu.VMEM((rows + 8, width), F32),
            pltpu.VMEM((rows + 8, width), F32),
            pltpu.VMEM((2, cells, width), BF16),
            pltpu.VMEM((cells, LANES), F32),
            pltpu.VMEM((8, WIDTH), F32),
            pltpu.VMEM((cells, LATENT), F32),
            pltpu.VMEM((rows + 8, LATENT), F32),
            pltpu.VMEM((rows + 8, LATENT), BF16),
            pltpu.VMEM((3, rows, LANES), F32),
            pltpu.VMEM((2, WIDTH // LANES, rows, LANES), F32),
            *latent_in,
            *coder_ring,
            *cells_ring,
            dma((2,)),
        ],
        compiler_params=params,
        name="second",
    )(
        blocks, flags, density, left, right, inflow, coder, w_latent, b_latent, restitution,
        *spread(message),
    )

    return pl.pallas_call(
        functools.partial(third_kernel, nb, peers),
        out_shape=shape((cells, vels), BF16),
        in_specs=[smem, hbm, hbm, hbm, vmem, vmem, vmem] + [vmem] * peers,
        out_specs=hbm,
        scratch_shapes=[
            pltpu.VMEM((cells, width), F32),
            pltpu.VMEM((cells, width), F32),
            pltpu.VMEM((2, cells, width), BF16),
            pltpu.VMEM((8, WIDTH), F32),
            pltpu.VMEM((cells + 8, LATENT), F32),
            pltpu.VMEM((cells + 8, LATENT), BF16),
            pltpu.VMEM((3, cells, LANES), F32),
            pltpu.VMEM((2, WIDTH // LANES, cells, LANES), F32),
            *latent_in,
            *coder_ring,
            *cells_ring,
            dma((2,)),
        ],
        compiler_params=params,
        name="third",
    )(blocks, coarse, coder, w_latent, b_latent, moments, restitution, *spread(message))


def solution(mesh):
    return jax.shard_map(
        body,
        mesh=mesh,
        in_specs=(
            P(("groups", "cell", "sub"), "vel"),
            P("vel", None),
            P(),
            P(),
            P(("groups", "cell", "sub")),
            P(("groups", "vel")),
            P("groups"),
            P(("groups", "vel")),
        ),
        out_specs=P(("groups", "cell", "sub"), "vel"),
        check_vma=False,
    )
```

time: 115 us -> 104 us (0.904)
  starting transfers between devices: 19 us -> 11.3 us
  other arithmetic: 2.89 us -> 1.17 us
  Pallas kernels: 64.8 us -> 63.6 us
    ppermute x14 -> x8, starting transfers between devices: 19 us -> 11.3 us  [shifted(): lax.ppermute(array, axes, [(i, (i + shift) % count) for i in range(count)])]
    add x2 -> x0, other arithmetic: 1.72 us -> none  [exchange(): total = total + shifted(messages[s], 'vel', count, s)]
    pallas_call x3, Pallas kernels: 64.8 us -> 63.6 us  [the longest x1 30.4 us: body(): pl.pallas_call(functools.partial(second_kernel, nb, peers), out_shape=(sh...]
    ppermute x14 -> x8, waiting for transfers between devices: 23.9 us -> 23.7 us  [shifted(): lax.ppermute(array, axes, [(i, (i + shift) % count) for i in range(count)])]
  transfers between devices with their start and end apart: 14 -> 8, of which waited for: 13 -> 6; matrix products, arithmetic and copies ran while one was open for 0% -> 0% of each run, Pallas kernels for 0% -> 0%
where the time goes in v3:
time: 104 us
  Pallas kernels  63.6 us (61%)
  waiting for transfers between devices  23.7 us (23%)
  starting transfers between devices  11.3 us (11%)
  local copies, waits for them, and re-layouts  4.01 us (4%)
  other arithmetic  1.17 us (1%)
    pallas_call x1, Pallas kernels, body(): pl.pallas_call(functools.partial(second_kernel, nb, peers), out_shape=(sh...  30.4 us
    ppermute x8, waiting for transfers between devices, shifted(): lax.ppermute(array, axes, [(i, (i + shift) % count) for i in range(count)])  23.7 us
    pallas_call x1, Pallas kernels, body(): pl.pallas_call(functools.partial(third_kernel, nb, peers), out_shape=shap...  17.8 us
    pallas_call x1, Pallas kernels, body(): pl.pallas_call(functools.partial(first_kernel, nb), out_shape=shape((rows...  15.4 us
    ppermute x8, starting transfers between devices, shifted(): lax.ppermute(array, axes, [(i, (i + shift) % count) for i in range(count)])  11.3 us
  transfers between devices with their start and end apart: 8, of which 6 were waited for; matrix products, arithmetic and copies ran while one was open for 0% of the time, Pallas kernels for 0%

profile of v3, /device:TPU:0, one launch (start us, length us, event | category | flops | bytes accessed | tf_op | source)
XLA Modules:
  0.0 104.0 jit_solution(17109153897339091484)
XLA Ops:
  0.0 0.8 fusion.14
  0.8 0.1 copy.11
  0.9 0.1 copy.10
  1.0 0.1 copy.9
  1.1 1.3 %fusion.18 = (bf16[4,27648]{1,0:T(4,128)(2,1)S(1)}, bf16[4,27648]{1,0:T(4,128)(2,1)S(1)}) fusion(bf16[96,27648]{1,0:T(8,128)(2,1)} %density.3), kind=kLoop, calls=%fused_computation.29 | loop fusion | bytes 884736 | tf_op jit(solution)/shard_map/slice | solution.py:539
  2.5 0.1 fusion.7
  2.5 0.1 pad_maximum_fusion
  2.6 0.5 collective-permute-start
  3.2 0.1 copy.12
  3.3 0.1 copy.14
  3.4 0.1 copy.13
  3.5 0.1 fusion.9
  3.6 0.1 pad_maximum_fusion.1
  3.7 2.0 %collective-permute-start.1 = (bf16[4,27776]{1,0:T(4,128)(2,1)S(1)}, bf16[4,27776]{1,0:T(4,128)(2,1)S(1)}, u32[]{:S(2)}, u32[]{:S(2)}) collective-permute-start(bf16[4,27776]{1,0:T(4,128)(2,1)S(1)} %pad_maximum_fusion.1), channel_id=1, source_target_pairs={{0,3},{1,0},{2,1},{3,2},{4,7},{5,4},{6,5},{7,6},{8,11},{9,8},{10,9... | collective-permute-start | bytes 666632 | tf_op jit(solution)/shard_map/ppermute | solution.py:508
  5.7 3.1 %collective-permute-done.left = bf16[4,27776]{1,0:T(4,128)(2,1)S(1)} collective-permute-done((bf16[4,27776]{1,0:T(4,128)(2,1)S(1)}, bf16[4,27776]{1,0:T(4,128)(2,1)S(1)}, u32[]{:S(2)}, u32[]{:S(2)}) %collective-permute-start) | collective-permute-done | bytes 222240 | tf_op jit(solution)/shard_map/ppermute | solution.py:508
  8.7 2.2 %collective-permute-done.1.right = bf16[4,27776]{1,0:T(4,128)(2,1)S(1)} collective-permute-done((bf16[4,27776]{1,0:T(4,128)(2,1)S(1)}, bf16[4,27776]{1,0:T(4,128)(2,1)S(1)}, u32[]{:S(2)}, u32[]{:S(2)}) %collective-permute-start.1) | collective-permute-done | bytes 222240 | tf_op jit(solution)/shard_map/ppermute | solution.py:508
  10.9 0.7 copy-done.1
  11.6 15.4 %first.1.refs_0_ = bf16[112,512]{1,0:T(8,128)(2,1)} custom-call(s32[24]{0:T(128)} %blocks.5, s32[4]{0:T(128)} %flags.3, bf16[96,27648]{1,0:T(8,128)(2,1)} %density.3, bf16[4,27776]{1,0:T(4,128)(2,1)} %copy-done, bf16[4,27776]{1,0:T(4,128)(2,1)} %copy-done.1, f32[1,27648]{1,0:T(1,128)} %bitcast.15, bf16[27648,512]{1,0:T(8,128)(2,1)} %coder.5), custom_call_target="tpu_custom_call" | custom-call | tf_op jit(solution)/shard_map/first/pallas_call | solution.py:554
  27.0 3.6 %collective-permute-start.4 = (bf16[112,512]{1,0:T(8,128)(2,1)}, bf16[112,512]{1,0:T(8,128)(2,1)S(1)}, u32[]{:S(2)}, u32[]{:S(2)}) collective-permute-start(bf16[112,512]{1,0:T(8,128)(2,1)} %first.1.refs_0_), channel_id=1, source_target_pairs={{0,12},{4,0},{8,4},{12,8},{1,13},{5,1},{9,5},{13,9},{2,14},{6,2},{... | collective-permute-start | bytes 344072 | tf_op jit(solution)/shard_map/ppermute | solution.py:508
  30.7 1.0 collective-permute-start.2
  31.7 2.9 %collective-permute-done.4.refs_3_ = bf16[112,512]{1,0:T(8,128)(2,1)S(1)} collective-permute-done((bf16[112,512]{1,0:T(8,128)(2,1)}, bf16[112,512]{1,0:T(8,128)(2,1)S(1)}, u32[]{:S(2)}, u32[]{:S(2)}) %collective-permute-start.4) | collective-permute-done | bytes 114720 | tf_op jit(solution)/shard_map/ppermute | solution.py:508
  34.6 7.7 %collective-permute-done.3.refs_2_ = bf16[112,512]{1,0:T(8,128)(2,1)S(1)} collective-permute-done((bf16[112,512]{1,0:T(8,128)(2,1)}, bf16[112,512]{1,0:T(8,128)(2,1)S(1)}, u32[]{:S(2)}, u32[]{:S(2)}) %collective-permute-start.3) | collective-permute-done | bytes 114720 | tf_op jit(solution)/shard_map/ppermute | solution.py:508
  42.3 0.6 copy-done.3
  43.0 30.4 %second.1 = (bf16[96,27648]{1,0:T(8,128)(2,1)}, bf16[104,512]{1,0:T(8,128)(2,1)}, f32[8,512]{1,0:T(8,128)}) custom-call(s32[24]{0:T(128)} %blocks.5, s32[4]{0:T(128)} %flags.3, bf16[96,27648]{1,0:T(8,128)(2,1)} %density.3, bf16[4,27776]{1,0:T(4,128)(2,1)} %copy-done, bf16[4,27776]{1,0:T(4,128)(2,1)} %copy-done.1, f32[1,27648]{1,0:T(1,128)} %bitcast.16, ...), custom_call_target="tpu_custom_call" | custom-call | tf_op jit(solution)/shard_map/second/pallas_call | solution.py:573
  73.4 1.0 collective-permute-start.7
  74.4 1.2 %collective-permute-start.6 = (bf16[104,512]{1,0:T(8,128)(2,1)}, bf16[104,512]{1,0:T(8,128)(2,1)S(1)}, u32[]{:S(2)}, u32[]{:S(2)}) collective-permute-start(bf16[104,512]{1,0:T(8,128)(2,1)} %get-tuple-element.10.refs_0_), channel_id=1, source_target_pairs={{0,8},{4,12},{8,0},{12,4},{1,9},{5,13},{9,1},{13,5},{2,10},{6,14},... | collective-permute-start | bytes 319496 | tf_op jit(solution)/shard_map/ppermute | solution.py:508
  75.6 1.9 %collective-permute-start.5 = (bf16[104,512]{1,0:T(8,128)(2,1)}, bf16[104,512]{1,0:T(8,128)(2,1)S(1)}, u32[]{:S(2)}, u32[]{:S(2)}) collective-permute-start(bf16[104,512]{1,0:T(8,128)(2,1)} %get-tuple-element.10.refs_0_), channel_id=1, source_target_pairs={{0,4},{4,8},{8,12},{12,0},{1,5},{5,9},{9,13},{13,1},{2,6},{6,10},{... | collective-permute-start | bytes 319496 | tf_op jit(solution)/shard_map/ppermute | solution.py:508
  77.5 1.4 %collective-permute-done.7.refs_3_ = bf16[104,512]{1,0:T(8,128)(2,1)S(1)} collective-permute-done((bf16[104,512]{1,0:T(8,128)(2,1)}, bf16[104,512]{1,0:T(8,128)(2,1)S(1)}, u32[]{:S(2)}, u32[]{:S(2)}) %collective-permute-start.7) | collective-permute-done | bytes 106528 | tf_op jit(solution)/shard_map/ppermute | solution.py:508
  79.0 6.4 %collective-permute-done.6.refs_2_ = bf16[104,512]{1,0:T(8,128)(2,1)S(1)} collective-permute-done((bf16[104,512]{1,0:T(8,128)(2,1)}, bf16[104,512]{1,0:T(8,128)(2,1)S(1)}, u32[]{:S(2)}, u32[]{:S(2)}) %collective-permute-start.6) | collective-permute-done | bytes 106528 | tf_op jit(solution)/shard_map/ppermute | solution.py:508
  85.4 0.6 copy-done.6
  86.0 0.0 copy-done.7
  86.1 17.8 %third.1 = bf16[96,27648]{1,0:T(8,128)(2,1)} custom-call(s32[24]{0:T(128)} %blocks.5, bf16[96,27648]{1,0:T(8,128)(2,1)} %get-tuple-element.8.source, bf16[27648,512]{1,0:T(8,128)(2,1)} %coder.5, bf16[512,512]{1,0:T(8,128)(2,1)} %w_latent.3, f32[1,512]{1,0:T(1,128)} %bitcast.18, f32[8,512]{1,0:T(8,128)} %get-tuple-element.9.moments, f32[1,96]{1,0:T(1,128)} %bitcast.20, ...), custom_call_target="tpu_custom_call" | custom-call | tf_op jit(solution)/shard_map/third/pallas_call | solution.py:605
  (15 shorter events, 0.0 us)
Async XLA Ops:
  2.6 6.1 %collective-permute-start = (bf16[4,27776]{1,0:T(4,128)(2,1)S(1)}, bf16[4,27776]{1,0:T(4,128)(2,1)S(1)}, u32[]{:S(2)}, u32[]{:S(2)}) collective-permute-start(bf16[4,27776]{1,0:T(4,128)(2,1)S(1)} %pad_maximum_fusion), channel_id=1, source_target_pairs={{0,1},{1,2},{2,3},{3,0},{4,5},{5,6},{6,7},{7,4},{8,9},{9,10},{10,1... | collective-permute-start | bytes 666632 | tf_op jit(solution)/shard_map/ppermute | solution.py:508
  3.7 7.2 %collective-permute-start.1 = (bf16[4,27776]{1,0:T(4,128)(2,1)S(1)}, bf16[4,27776]{1,0:T(4,128)(2,1)S(1)}, u32[]{:S(2)}, u32[]{:S(2)}) collective-permute-start(bf16[4,27776]{1,0:T(4,128)(2,1)S(1)} %pad_maximum_fusion.1), channel_id=1, source_target_pairs={{0,3},{1,0},{2,1},{3,2},{4,7},{5,4},{6,5},{7,6},{8,11},{9,8},{10,9... | collective-permute-start | bytes 666632 | tf_op jit(solution)/shard_map/ppermute | solution.py:508
  8.7 2.2 %copy-start = (bf16[4,27776]{1,0:T(4,128)(2,1)}, bf16[4,27776]{1,0:T(4,128)(2,1)S(1)}, u32[]{:S(2)}) copy-start(bf16[4,27776]{1,0:T(4,128)(2,1)S(1)} %collective-permute-done.left) | copy-start | bytes 666628
  10.9 0.7 copy-start.1
  27.0 7.5 %collective-permute-start.4 = (bf16[112,512]{1,0:T(8,128)(2,1)}, bf16[112,512]{1,0:T(8,128)(2,1)S(1)}, u32[]{:S(2)}, u32[]{:S(2)}) collective-permute-start(bf16[112,512]{1,0:T(8,128)(2,1)} %first.1.refs_0_), channel_id=1, source_target_pairs={{0,12},{4,0},{8,4},{12,8},{1,13},{5,1},{9,5},{13,9},{2,14},{6,2},{... | collective-permute-start | bytes 344072 | tf_op jit(solution)/shard_map/ppermute | solution.py:508
  30.7 11.6 %collective-permute-start.3 = (bf16[112,512]{1,0:T(8,128)(2,1)}, bf16[112,512]{1,0:T(8,128)(2,1)S(1)}, u32[]{:S(2)}, u32[]{:S(2)}) collective-permute-start(bf16[112,512]{1,0:T(8,128)(2,1)} %first.1.refs_0_), channel_id=1, source_target_pairs={{0,8},{4,12},{8,0},{12,4},{1,9},{5,13},{9,1},{13,5},{2,10},{6,14},... | collective-permute-start | bytes 344072 | tf_op jit(solution)/shard_map/ppermute | solution.py:508
  30.7 11.6 %collective-permute-start.2 = (bf16[112,512]{1,0:T(8,128)(2,1)}, bf16[112,512]{1,0:T(8,128)(2,1)S(1)}, u32[]{:S(2)}, u32[]{:S(2)}) collective-permute-start(bf16[112,512]{1,0:T(8,128)(2,1)} %first.1.refs_0_), channel_id=1, source_target_pairs={{0,4},{4,8},{8,12},{12,0},{1,5},{5,9},{9,13},{13,1},{2,6},{6,10},{... | collective-permute-start | bytes 344072 | tf_op jit(solution)/shard_map/ppermute | solution.py:508
  34.6 7.7 %copy-start.2 = (bf16[112,512]{1,0:T(8,128)(2,1)}, bf16[112,512]{1,0:T(8,128)(2,1)S(1)}, u32[]{:S(2)}) copy-start(bf16[112,512]{1,0:T(8,128)(2,1)S(1)} %collective-permute-done.4.refs_3_) | copy-start | bytes 344068
  42.3 0.7 copy-start.3
  42.3 0.7 copy-start.4
  73.4 5.6 %collective-permute-start.7 = (bf16[104,512]{1,0:T(8,128)(2,1)}, bf16[104,512]{1,0:T(8,128)(2,1)S(1)}, u32[]{:S(2)}, u32[]{:S(2)}) collective-permute-start(bf16[104,512]{1,0:T(8,128)(2,1)} %get-tuple-element.10.refs_0_), channel_id=1, source_target_pairs={{0,12},{4,0},{8,4},{12,8},{1,13},{5,1},{9,5},{13,9},{2,14},{6,2},{... | collective-permute-start | bytes 319496 | tf_op jit(solution)/shard_map/ppermute | solution.py:508
  74.4 11.0 %collective-permute-start.6 = (bf16[104,512]{1,0:T(8,128)(2,1)}, bf16[104,512]{1,0:T(8,128)(2,1)S(1)}, u32[]{:S(2)}, u32[]{:S(2)}) collective-permute-start(bf16[104,512]{1,0:T(8,128)(2,1)} %get-tuple-element.10.refs_0_), channel_id=1, source_target_pairs={{0,8},{4,12},{8,0},{12,4},{1,9},{5,13},{9,1},{13,5},{2,10},{6,14},... | collective-permute-start | bytes 319496 | tf_op jit(solution)/shard_map/ppermute | solution.py:508
  75.6 9.8 %collective-permute-start.5 = (bf16[104,512]{1,0:T(8,128)(2,1)}, bf16[104,512]{1,0:T(8,128)(2,1)S(1)}, u32[]{:S(2)}, u32[]{:S(2)}) collective-permute-start(bf16[104,512]{1,0:T(8,128)(2,1)} %get-tuple-element.10.refs_0_), channel_id=1, source_target_pairs={{0,4},{4,8},{8,12},{12,0},{1,5},{5,9},{9,13},{13,1},{2,6},{6,10},{... | collective-permute-start | bytes 319496 | tf_op jit(solution)/shard_map/ppermute | solution.py:508
  79.0 6.4 %copy-start.5 = (bf16[104,512]{1,0:T(8,128)(2,1)}, bf16[104,512]{1,0:T(8,128)(2,1)S(1)}, u32[]{:S(2)}) copy-start(bf16[104,512]{1,0:T(8,128)(2,1)S(1)} %collective-permute-done.7.refs_3_) | copy-start | bytes 319492
  85.4 0.7 copy-start.6
  85.4 0.7 copy-start.7
